TPU v7x, 32 devices: a whole 2x2x4 slice. The times are simulated.
32 devices in a mesh: stn: 2 (over x), tm: 16 (over z, y, core).
Axes of the slice: x: 2, y: 2, z: 4, core: 2. Of those that a mesh axis runs over, the one named last changes fastest.
Arguments:
- spectra: bfloat16 [16, 8, 64, 2, 4096], P('stn', None, 'tm'), may hold values from -6 to 6
- flags: int32 [16, 8, 64, 32], P('stn', None, 'tm'), may hold values from 0 to 1, as said below
- poly_index: int32 [16, 8, 64], P('stn', None, 'tm'), may hold values from 0 to 63
- delay_model: float32 [64, 3], replicated, may hold values from -48 to 48
- partner_order: int32 [16], replicated, may hold values from 0 to 15, each once
Outputs:
- fringe: float32 [2, 256, 8, 256], P(None, ('stn', 'tm'))
Inputs may be any that keep to these rules, and one draw needn't show every extreme that they name: `flags`: 1 marks a flagged block; whole blocks of a station can be flagged for the full window. `partner_order`: each station appears once.
All inputs are finite; a program needn't handle non-finite values.
Results may differ from a plain program's by a relative error of at most 0.003.
Values may be sent and summed in bfloat16 or wider, within the bound.
A program may use at most 128 MiB of HBM per device.

v0:
```python
import functools
import math

import jax
import jax.numpy as jnp
import numpy as np
from jax import lax
from jax.experimental import pallas as pl
from jax.experimental.pallas import tpu as pltpu
from jax.sharding import PartitionSpec as P

LAGS = 256
QUARTERS = 4
LANES = 128


def lag_tables(channels):
    lags = np.arange(1, LAGS // 2 + 1)
    j = np.arange(channels // QUARTERS)
    angle = (j[:, None] * lags[None, :] % channels) * (2.0 * np.pi / channels)
    table = np.concatenate([np.cos(angle), np.sin(angle)], axis=1).astype(np.float32)
    high = table.astype(jnp.bfloat16)
    low = (table - high.astype(np.float32)).astype(jnp.bfloat16)
    return high, low


def split(value):
    high = value.astype(jnp.bfloat16)
    low = (value - high.astype(jnp.float32)).astype(jnp.bfloat16)
    return high, low


def dot(a, b):
    return jnp.dot(a, b, preferred_element_type=jnp.float32)


def correlate_kernel(x_ref, e1_ref, e2_ref, scale_ref, wh_ref, wl_ref, pick_ref, out_ref, y_ref, vh_ref, vl_ref, z_ref):
    depth, _, stations, width = x_ref.shape[1:]
    half = stations // 2
    blocks = width // LANES
    quarter = pl.program_id(1)

    def put(row, col, value):
        high, low = split(value)
        cols = slice(col * LANES, (col + 1) * LANES)
        vh_ref[row : row + stations, cols] = high
        vl_ref[row : row + stations, cols] = low

    for h in range(blocks):
        cols = slice(h * LANES, (h + 1) * LANES)
        slot = h % 2
        mine = []
        for k in range(depth):
            c1 = e1_ref[0, 0, k, 0, :, h : h + 1]
            s1 = e1_ref[0, 0, k, 1, :, h : h + 1]
            c2 = e2_ref[0, k, 0]
            s2 = e2_ref[0, k, 1]
            cosine = c1 * c2 - s1 * s2
            sine = s1 * c2 + c1 * s2
            real = x_ref[0, k, 0, :, cols].astype(jnp.float32)
            imag = x_ref[0, k, 1, :, cols].astype(jnp.float32)
            new_real = (real * cosine + imag * sine).astype(jnp.bfloat16).astype(jnp.float32)
            new_imag = (imag * cosine - real * sine).astype(jnp.bfloat16).astype(jnp.float32)
            y_ref[slot, k, 0, :stations] = new_real
            y_ref[slot, k, 1, :stations] = new_imag
            y_ref[slot, k, 0, stations:] = new_real[:half]
            y_ref[slot, k, 1, stations:] = new_imag[:half]
            mine.append((new_real, new_imag))
        for d in range(half + 1):
            count = half if d == half else stations
            real = None
            imag = None
            for k in range(depth):
                ar, ai = mine[k]
                ar, ai = ar[:count], ai[:count]
                if d == 0:
                    br, bi = ar, ai
                else:
                    br = y_ref[slot, k, 0, d : d + count]
                    bi = y_ref[slot, k, 1, d : d + count]
                term = ar * br + ai * bi
                real = term if real is None else real + term
                if d > 0:
                    term = ai * br - ar * bi
                    imag = term if imag is None else imag + term
            scale = scale_ref[0, 0, d * stations : d * stations + count, h : h + 1]
            if d == half:
                both = jnp.concatenate([real * scale, imag * scale], axis=0)
                put(stations * (stations - 1), h, both)
            else:
                put(d * stations, h, real * scale)
                if d > 0:
                    put((half + d - 1) * stations, h, imag * scale)

    vh = vh_ref[...]
    part = dot(vh, wh_ref[...]) + dot(vh, wl_ref[...]) + dot(vl_ref[...], wh_ref[...])
    lags = part.shape[1] // 2
    part_c = part[:, :lags]
    part_s = part[:, lags:]
    lag = lax.broadcasted_iota(jnp.int32, part_c.shape, 1) + 1
    turn = (lag * quarter) % 4
    cq = jnp.where(turn == 0, 1.0, jnp.where(turn == 2, -1.0, 0.0))
    sq = jnp.where(turn == 1, 1.0, jnp.where(turn == 3, -1.0, 0.0))
    new_c = part_c * cq - part_s * sq
    new_s = part_s * cq + part_c * sq

    @pl.when(quarter == 0)
    def _():
        z_ref[:, :lags] = new_c
        z_ref[:, lags:] = new_s

    @pl.when(quarter > 0)
    def _():
        z_ref[:, :lags] += new_c
        z_ref[:, lags:] += new_s

    @pl.when(quarter == QUARTERS - 1)
    def _():
        z = z_ref[...]
        high = z.astype(jnp.bfloat16)
        rest = z - high.astype(jnp.float32)
        mid, low = split(rest)
        pick = pick_ref[...]
        rows = dot(pick, high) + dot(pick, mid) + dot(pick, low)
        out_ref[...] = rows.reshape(out_ref.shape)


def correlate(x, e1, e2, scale, high, low, pick, owners):
    periods, depth, _, stations, channels = x.shape
    width = channels // QUARTERS
    rows = stations * stations
    return pl.pallas_call(
        correlate_kernel,
        grid=(periods, QUARTERS),
        in_specs=[
            pl.BlockSpec((1, depth, 2, stations, width), lambda p, q: (p, 0, 0, 0, q)),
            pl.BlockSpec((1, 1) + e1.shape[2:], lambda p, q: (p, q, 0, 0, 0, 0)),
            pl.BlockSpec((1,) + e2.shape[1:], lambda p, q: (p, 0, 0, 0, 0)),
            pl.BlockSpec((1, 1) + scale.shape[2:], lambda p, q: (p, q, 0, 0)),
            pl.BlockSpec(high.shape, lambda p, q: (0, 0)),
            pl.BlockSpec(low.shape, lambda p, q: (0, 0)),
            pl.BlockSpec(pick.shape, lambda p, q: (0, 0)),
        ],
        out_specs=pl.BlockSpec((owners, 1, 2 * rows // owners, LAGS), lambda p, q: (0, p, 0, 0)),
        out_shape=jax.ShapeDtypeStruct((owners, periods, 2 * rows // owners, LAGS), jnp.float32),
        scratch_shapes=[
            pltpu.VMEM((2, depth, 2, stations + stations // 2, LANES), jnp.float32),
            pltpu.VMEM((rows, width), jnp.bfloat16),
            pltpu.VMEM((rows, width), jnp.bfloat16),
            pltpu.VMEM((rows, LAGS), jnp.float32),
        ],
        compiler_params=pltpu.CompilerParams(dimension_semantics=("arbitrary", "arbitrary")),
        name="correlate",
    )(x, e1, e2, scale, high, low, pick)


def finish_kernel(factor, g_ref, pc_ref, ps_ref, out_ref):
    highest = lax.Precision.HIGHEST
    lags = g_ref.shape[-1] // 2
    rc, rs = g_ref[0, :, :lags], g_ref[0, :, lags:]
    ic, im_s = g_ref[1, :, :lags], g_ref[1, :, lags:]
    flip = (
        lax.broadcasted_iota(jnp.int32, (lags, lags), 0) + lax.broadcasted_iota(jnp.int32, (lags, lags), 1) == lags - 1
    ).astype(jnp.float32)
    pcos = pc_ref[...]
    psin = ps_ref[...]

    def mix(m, v):
        return jnp.dot(m, v, precision=highest, preferred_element_type=jnp.float32)

    for side in range(2):
        if side == 0:
            real, imag = mix(rc - im_s, flip), mix(ic + rs, flip)
        else:
            real, imag = rc + im_s, ic - rs
        cols = slice(side * lags, (side + 1) * lags)
        out_ref[0, :, cols] = (mix(pcos, real) + mix(psin, imag)) * factor
        out_ref[1, :, cols] = (mix(pcos, imag) - mix(psin, real)) * factor


def finish(g, periods, channels):
    rows = g.shape[1] // periods
    idx = np.arange(periods)
    angle = (idx[:, None] * idx[None, :] % periods) * (2.0 * np.pi / periods)
    eye = np.eye(rows)

    def table(m):
        wide = np.einsum("rp,nm->nrpm", m, eye).reshape(rows * periods, periods * rows)
        return jnp.asarray(wide.astype(np.float32))

    out = pl.pallas_call(
        functools.partial(finish_kernel, 1.0 / math.sqrt(periods * channels)),
        out_shape=jax.ShapeDtypeStruct((2, rows * periods, LAGS), jnp.float32),
        name="finish",
    )(g, table(np.cos(angle)), table(np.sin(angle)))
    return out.reshape(2, rows, periods, LAGS)


def pick_matrix(partner_order, stations, first_station, groups, owners):
    half = stations // 2
    own_rows = stations * stations // (groups * owners)
    n = np.arange(stations * stations).reshape(groups, owners, own_rows).transpose(1, 0, 2)
    a = jnp.asarray(n // stations, jnp.int32)
    onehot = (jnp.asarray(n % stations, jnp.int32)[..., None] == jnp.arange(stations)).astype(jnp.int32)
    b = jnp.sum(onehot * partner_order, axis=-1)
    a = (a - first_station) % stations
    b = (b - first_station) % stations
    d = (b - a) % stations
    flip = (d > half) | ((d == half) & (a >= half))
    d = jnp.where(flip, (stations - d) % stations, d)
    row = jnp.where(flip, b, a)
    top = stations * (stations - 1)
    real_col = jnp.where(d == half, top + row, d * stations + row)
    imag_col = jnp.where(d == half, top + half + row, (half + d - 1) * stations + row)
    imag_col = jnp.where(d == 0, -1, imag_col)
    sign = jnp.where(flip, -1.0, 1.0)
    col = jnp.stack([real_col, imag_col], axis=2)
    value = jnp.stack([jnp.ones_like(sign), sign], axis=2)
    pick = jnp.where(col[..., None] == jnp.arange(stations * stations), value[..., None], 0.0)
    return pick.reshape(2 * stations * stations, stations * stations).astype(jnp.bfloat16)


def per_device(spectra, flags, poly_index, delay_model, partner_order):
    local, periods, depth, _, channels = spectra.shape
    groups = lax.axis_size("stn")
    owners = lax.axis_size("tm")
    me = lax.axis_index("stn")
    stations = local * groups
    mine = periods // groups
    blocks = flags.shape[-1]
    first_station = (me + 1) % groups * local

    chunks = []
    for i in range(mine):
        pieces = []
        for shift in range(groups - 1, -1, -1):
            target = (me + shift) % groups
            piece = lax.dynamic_slice_in_dim(spectra, target * mine + i, 1, axis=1)
            if shift:
                piece = lax.ppermute(piece, "stn", [(g, (g + shift) % groups) for g in range(groups)])
            pieces.append(piece)
        chunks.append(jnp.concatenate(pieces, axis=0).transpose(1, 2, 3, 0, 4))

    ints = jnp.concatenate([flags, poly_index[..., None]], axis=-1)
    ints = lax.all_to_all(ints, "stn", split_axis=1, concat_axis=0, tiled=True)
    ints = jnp.roll(ints, -first_station, axis=0)
    weight = 1.0 - ints[..., :blocks].astype(jnp.float32)
    index = ints[..., blocks]

    pairs = jnp.stack([weight * jnp.roll(weight, -d, axis=0) for d in range(stations // 2 + 1)])
    counts = jnp.sum(pairs, axis=3).reshape((stations // 2 + 1) * stations, mine, blocks)
    counts = lax.psum(counts.astype(jnp.bfloat16), "tm").astype(jnp.float32)
    scale = 1.0 / jnp.sqrt(jnp.maximum(counts, 1.0))
    scale = scale.reshape(scale.shape[0], mine, QUARTERS, blocks // QUARTERS).transpose(1, 2, 0, 3)

    total = depth * owners
    times = (
        (me * mine + jnp.arange(mine, dtype=jnp.int32))[:, None] * total
        + lax.axis_index("tm") * depth
        + jnp.arange(depth, dtype=jnp.int32)[None, :]
    ).astype(jnp.float32)
    moment = times / float(periods * total)
    table_rows = delay_model.shape[0]
    onehot = (index[..., None] == jnp.arange(table_rows, dtype=jnp.int32)).astype(jnp.float32)
    coeffs = jnp.dot(onehot.reshape(-1, table_rows), delay_model, precision=lax.Precision.HIGHEST)
    coeffs = coeffs.reshape(stations, mine, depth, 3)
    delay = coeffs[..., 0] + coeffs[..., 1] * moment + coeffs[..., 2] * moment * moment
    step = math.pi / channels
    coarse = delay[..., None] * (jnp.arange(blocks, dtype=jnp.int32).astype(jnp.float32) * (step * (channels // blocks)))
    fine = delay[..., None] * (jnp.arange(channels // blocks, dtype=jnp.int32).astype(jnp.float32) * step)
    e1 = jnp.stack([weight * jnp.cos(coarse), weight * jnp.sin(coarse)], axis=3)
    e1 = e1.reshape(stations, mine, depth, 2, QUARTERS, blocks // QUARTERS).transpose(1, 4, 2, 3, 0, 5)
    e2 = jnp.stack([jnp.cos(fine), jnp.sin(fine)], axis=3).transpose(1, 2, 3, 0, 4)

    high, low = lag_tables(channels)
    high, low = jnp.asarray(high), jnp.asarray(low)
    pick = pick_matrix(partner_order, stations, first_station, groups, owners)
    done = []
    for i in range(mine):
        part = correlate(chunks[i], e1[i : i + 1], e2[i : i + 1], scale[i : i + 1], high, low, pick, owners)
        done.append(lax.psum_scatter(part, "tm", scatter_dimension=0, tiled=True)[0])
    own = jnp.concatenate(done, axis=0)
    own = own.reshape(mine, groups, 2, -1, LAGS)
    own = lax.all_to_all(own, "stn", split_axis=1, concat_axis=0, tiled=True)
    own = own.reshape(periods, 2, -1, LAGS).transpose(1, 0, 2, 3).reshape(2, -1, LAGS)
    return finish(own, periods, channels)


def solution(mesh):
    return jax.shard_map(
        per_device,
        mesh=mesh,
        in_specs=(
            P("stn", None, "tm", None, None),
            P("stn", None, "tm", None),
            P("stn", None, "tm"),
            P(),
            P(),
        ),
        out_specs=P(None, ("stn", "tm"), None, None),
        check_vma=False,
    )
```

profile of v0, /device:TPU:0, one launch (start us, length us, event | category | flops | bytes accessed | tf_op | source)
XLA Modules:
  0.0 357.1 jit_solution(2376357880272823090)
XLA Ops:
  6.5 1.0 copy.131
  7.5 1.0 copy.132
  8.6 0.9 reshape.105
  9.5 4.2 %all-to-all-start = ((s32[2,1,4224]{2,1,0:T(1,128)}), s32[2,1,4224]{2,1,0:T(1,128)S(1)}, u32[]{:S(2)}, u32[]{:S(2)}) async-start(s32[2,1,4224]{2,1,0:T(1,128)} %reshape.105), calls=%async_computation | async-start | bytes 67584 | tf_op jit(solution)/shard_map/all_to_all | solution.py:245
  13.7 7.9 %constant_dynamic-slice_fusion.7 = (bf16[8,1,4,2,4096]{4,3,2,1,0:T(2,128)(2,1)S(1)}, bf16[8,1,4,2,4096]{4,3,2,1,0:T(2,128)(2,1)}, bf16[8,1,4,2,4096]{4,3,2,1,0:T...) fusion(bf16[8,8,4,2,4096]{4,3,2,1,0:T(2,128)(2,1)} %param.11, ...), kind=kLoop, calls=%fused_computation.92 | loop fusion | bytes 8388640 | tf_op jit(solution)/shard_map/dynamic_slice | solution.py:238
  21.6 1.1 copy.157
  22.7 2.1 collective-permute-start
  24.8 1.1 copy.159
  26.0 0.7 select_reduce_fusion
  27.3 0.9 select_convert_fusion.pick_ref
  28.2 0.3 copy.158
  28.6 0.5 broadcast.149
  29.1 0.7 reduce.2
  30.1 0.4 slice_reduce_fusion
  30.5 0.6 fusion.20
  31.3 0.5 fusion
  32.7 61.6 %psum.7 = bf16[144,4,32]{0,2,1:T(8,128)(2,1)S(1)} all-reduce(bf16[144,4,32]{0,2,1:T(8,128)(2,1)S(1)} %copy.139), channel_id=1, replica_groups=mesh['stn'=2,'tm'=16] {'tm'}, use_global_device_ids=true, to_apply=%region_1.2 | all-reduce | flops 18432 | bytes 73728 | tf_op jit(solution)/shard_map/psum | solution.py:252
  94.5 0.2 copy.136
  94.8 0.2 copy.137
  95.1 0.5 multiply_cosine_fusion
  95.7 0.7 fusion.34
  96.4 0.4 copy.140
  96.9 1.0 fusion.33
  97.9 1.1 fusion.32
  99.0 2.1 maximum_bitcast_fusion.x_ref
  101.1 9.1 %correlate.4 = f32[16,1,32,256]{3,2,1,0:T(8,128)} custom-call(bf16[1,4,2,16,4096]{4,3,2,1,0:T(8,128)(2,1)} %maximum_bitcast_fusion.x_ref, f32[1,4,4,2,16,8]{5,4,3,2,1,0:T(8,128)} %get-tuple-element.21.e1_ref, f32[1,4,2,16,128]{4,3,2,1,0:T(8,128)} %get-tuple-element.25.e2_ref, f32[1,4,144,8]{3,2,1,0:T(8,128)} %get-tuple-element.17.scale_ref, ...), custom_call_target="tpu_custom_call" | custom-call | tf_op jit(solution)/shard_map/correlate/pallas_call | solution.py:132
  110.2 0.2 reduce-scatter.7.cloned.1.call-start
  110.5 0.3 copy.161
  110.8 1.7 collective-permute-start.2
  112.4 0.3 copy.160
  112.7 2.1 maximum_bitcast_fusion.2.x_ref
  114.9 9.1 %correlate.5 = f32[16,1,32,256]{3,2,1,0:T(8,128)} custom-call(bf16[1,4,2,16,4096]{4,3,2,1,0:T(8,128)(2,1)} %maximum_bitcast_fusion.2.x_ref, f32[1,4,4,2,16,8]{5,4,3,2,1,0:T(8,128)} %get-tuple-element.24.e1_ref, f32[1,4,2,16,128]{4,3,2,1,0:T(8,128)} %get-tuple-element.28.e2_ref, f32[1,4,144,8]{3,2,1,0:T(8,128)} %get-tuple-element.20.scale_ref, ...), custom_call_target="tpu_custom_call" | custom-call | tf_op jit(solution)/shard_map/correlate/pallas_call | solution.py:132
  124.1 0.3 copy.163
  124.4 0.5 collective-permute-start.3
  125.0 0.3 copy.162
  125.3 1.0 maximum_bitcast_fusion.3.x_ref
  126.4 9.0 %correlate.6 = f32[16,1,32,256]{3,2,1,0:T(8,128)} custom-call(bf16[1,4,2,16,4096]{4,3,2,1,0:T(8,128)(2,1)} %maximum_bitcast_fusion.3.x_ref, f32[1,4,4,2,16,8]{5,4,3,2,1,0:T(8,128)} %get-tuple-element.23.e1_ref, f32[1,4,2,16,128]{4,3,2,1,0:T(8,128)} %get-tuple-element.27.e2_ref, f32[1,4,144,8]{3,2,1,0:T(8,128)} %get-tuple-element.19.scale_ref, ...), custom_call_target="tpu_custom_call" | custom-call | tf_op jit(solution)/shard_map/correlate/pallas_call | solution.py:132
  135.5 0.3 copy.164
  135.8 1.0 maximum_bitcast_fusion.4.x_ref
  136.8 9.0 %correlate.7 = f32[16,1,32,256]{3,2,1,0:T(8,128)} custom-call(bf16[1,4,2,16,4096]{4,3,2,1,0:T(8,128)(2,1)} %maximum_bitcast_fusion.4.x_ref, f32[1,4,4,2,16,8]{5,4,3,2,1,0:T(8,128)} %get-tuple-element.22.e1_ref, f32[1,4,2,16,128]{4,3,2,1,0:T(8,128)} %get-tuple-element.26.e2_ref, f32[1,4,144,8]{3,2,1,0:T(8,128)} %get-tuple-element.18.scale_ref, ...), custom_call_target="tpu_custom_call" | custom-call | tf_op jit(solution)/shard_map/correlate/pallas_call | solution.py:132
  145.8 18.0 %reduce-scatter.5.cloned.1.call-done = f32[1,1,32,256]{3,2,1,0:T(8,128)} async-done(((f32[16,1,32,256]{3,2,1,0:T(8,128)}), f32[1,1,32,256]{3,2,1,0:T(8,128)}) %reduce-scatter.5.cloned.1.call-update) | async-done | bytes 32784 | tf_op jit(solution)/shard_map/reduce_scatter | solution.py:281
  163.9 58.7 %reduce-scatter.7.cloned.1.call-done = f32[1,1,32,256]{3,2,1,0:T(8,128)} async-done(((f32[16,1,32,256]{3,2,1,0:T(8,128)}), f32[1,1,32,256]{3,2,1,0:T(8,128)}) %reduce-scatter.7.cloned.1.call-update) | async-done | bytes 32784 | tf_op jit(solution)/shard_map/reduce_scatter | solution.py:281
  222.6 58.7 %reduce-scatter.9.cloned.1.call-done = f32[1,1,32,256]{3,2,1,0:T(8,128)} async-done(((f32[16,1,32,256]{3,2,1,0:T(8,128)}), f32[1,1,32,256]{3,2,1,0:T(8,128)}) %reduce-scatter.9.cloned.1.call-update) | async-done | bytes 32784 | tf_op jit(solution)/shard_map/reduce_scatter | solution.py:281
  281.3 58.6 %reduce-scatter.11.cloned.1.call-done = f32[1,1,32,256]{3,2,1,0:T(8,128)} async-done(((f32[16,1,32,256]{3,2,1,0:T(8,128)}), f32[1,1,32,256]{3,2,1,0:T(8,128)}) %reduce-scatter.11.cloned.1.call-update) | async-done | bytes 32784 | tf_op jit(solution)/shard_map/reduce_scatter | solution.py:281
  340.0 0.8 pad_maximum_fusion
  340.8 7.0 %all_to_all.33 = f32[4,2,2,8,256]{4,3,2,0,1:T(8,128)S(1)} all-to-all(f32[4,2,2,8,256]{4,3,2,0,1:T(8,128)S(1)} %pad_maximum_fusion), channel_id=1, replica_groups=mesh['stn'=2,'tm'=16] {'stn'}, dimensions={1} | all-to-all | bytes 262144 | tf_op jit(solution)/shard_map/all_to_all | solution.py:284
  347.8 0.7 copy_bitcast_fusion.g_ref
  348.4 2.2 finish.1
  (78 shorter events, 2.6 us)
Async XLA Ops:
  6.5 24.0 %copy-start = (f32[64,3]{0,1:T(4,128)S(1)}, f32[64,3]{0,1:T(4,128)}, u32[]{:S(2)}) copy-start(f32[64,3]{0,1:T(4,128)} %param.14) | copy-start | bytes 2308
  9.5 19.1 %all-to-all-start = ((s32[2,1,4224]{2,1,0:T(1,128)}), s32[2,1,4224]{2,1,0:T(1,128)S(1)}, u32[]{:S(2)}, u32[]{:S(2)}) async-start(s32[2,1,4224]{2,1,0:T(1,128)} %reshape.105), calls=%async_computation | async-start | bytes 67584 | tf_op jit(solution)/shard_map/all_to_all | solution.py:245
  13.7 150.2 %reduce-scatter.5.cloned.1.call-start = ((), (), s32[]{:S(2)}) async-start(), calls=%async_computation.6 | async-start | bytes 557056 | tf_op jit(solution)/shard_map/reduce_scatter | solution.py:281
  21.6 4.4 %copy-start.5 = (s32[16,2,8]{2,1,0:T(2,128)S(1)}, s32[16,2,8]{2,1,0:T(2,128)}, u32[]{:S(2)}) copy-start(s32[16,2,8]{2,1,0:T(2,128)} %constant.149.clone) | copy-start | bytes 3076
  21.6 4.4 %copy-start.7 = (s32[16]{0:T(128)S(1)}, s32[16]{0:T(128)}, u32[]{:S(2)}) copy-start(s32[16]{0:T(128)} %param.15) | copy-start | bytes 196
  21.6 5.1 %copy-start.6 = (s32[16,2,8]{2,1,0:T(2,128)S(1)}, s32[16,2,8]{2,1,0:T(2,128)}, u32[]{:S(2)}) copy-start(s32[16,2,8]{2,1,0:T(2,128)} %constant.148.clone) | copy-start | bytes 3076
  22.7 76.3 %collective-permute-start = (bf16[8,1,4,2,4096]{4,0,3,2,1:T(8,128)(2,1)}, bf16[8,1,4,2,4096]{4,0,3,2,1:T(8,128)(2,1)}, u32[]{:S(2)}, u32[]{:S(2)}) collective-permute-start(bf16[8,1,4,2,4096]{4,0,3,2,1:T(8,128)(2,1)} %copy.157), channel_id=1, source_target_pairs={{0,16},{16,0},{1,17},{17,1},{2,18},{18,2},{3,19},{19,3},{4,20},{20... | collective-permute-start | bytes 1572872 | tf_op jit(solution)/shard_map/ppermute | solution.py:240
  25.9 86.8 %collective-permute-start.1 = (bf16[8,1,4,2,4096]{4,0,3,2,1:T(8,128)(2,1)}, bf16[8,1,4,2,4096]{4,0,3,2,1:T(8,128)(2,1)}, u32[]{:S(2)}, u32[]{:S(2)}) collective-permute-start(bf16[8,1,4,2,4096]{4,0,3,2,1:T(8,128)(2,1)} %copy.159), channel_id=1, source_target_pairs={{0,16},{16,0},{1,17},{17,1},{2,18},{18,2},{3,19},{19,3},{4,20},{20... | collective-permute-start | bytes 1572872 | tf_op jit(solution)/shard_map/ppermute | solution.py:240
  101.1 9.3 %copy-start.4 = (bf16[8,1,4,2,4096]{4,3,2,1,0:T(2,128)(2,1)S(1)}, bf16[8,1,4,2,4096]{4,3,2,1,0:T(2,128)(2,1)}, u32[]{:S(2)}) copy-start(bf16[8,1,4,2,4096]{4,3,2,1,0:T(2,128)(2,1)} %get-tuple-element.12) | copy-start | bytes 1572868
  110.2 2.2 copy-start.3
  110.2 112.4 %reduce-scatter.7.cloned.1.call-start = ((), (), s32[]{:S(2)}) async-start(), calls=%async_computation.7 | async-start | bytes 557056 | tf_op jit(solution)/shard_map/reduce_scatter | solution.py:281
  110.8 14.6 %collective-permute-start.2 = (bf16[8,1,4,2,4096]{4,0,3,2,1:T(8,128)(2,1)S(1)}, bf16[8,1,4,2,4096]{4,0,3,2,1:T(8,128)(2,1)S(1)}, u32[]{:S(2)}, u32[]{:S(2)}) collective-permute-start(bf16[8,1,4,2,4096]{4,0,3,2,1:T(8,128)(2,1)S(1)} %copy.161), channel_id=1, source_target_pairs={{0,16},{16,0},{1,17},{17,1},{2,18},{18,2},{3,19},{19,3},{4,20},{20... | collective-permute-start | bytes 1572872 | tf_op jit(solution)/shard_map/ppermute | solution.py:240
  114.9 9.2 %copy-start.2 = (bf16[8,1,4,2,4096]{4,3,2,1,0:T(2,128)(2,1)S(1)}, bf16[8,1,4,2,4096]{4,3,2,1,0:T(2,128)(2,1)}, u32[]{:S(2)}) copy-start(bf16[8,1,4,2,4096]{4,3,2,1,0:T(2,128)(2,1)} %get-tuple-element.10) | copy-start | bytes 1572868
  124.0 1.0 copy-start.1
  124.0 157.3 %reduce-scatter.9.cloned.1.call-start = ((), (), s32[]{:S(2)}) async-start(), calls=%async_computation.8 | async-start | bytes 557056 | tf_op jit(solution)/shard_map/reduce_scatter | solution.py:281
  124.4 11.4 %collective-permute-start.3 = (bf16[8,1,4,2,4096]{4,0,3,2,1:T(8,128)(2,1)S(1)}, bf16[8,1,4,2,4096]{4,0,3,2,1:T(8,128)(2,1)S(1)}, u32[]{:S(2)}, u32[]{:S(2)}) collective-permute-start(bf16[8,1,4,2,4096]{4,0,3,2,1:T(8,128)(2,1)S(1)} %copy.163), channel_id=1, source_target_pairs={{0,16},{16,0},{1,17},{17,1},{2,18},{18,2},{3,19},{19,3},{4,20},{20... | collective-permute-start | bytes 1572872 | tf_op jit(solution)/shard_map/ppermute | solution.py:240
  135.4 204.5 %reduce-scatter.11.cloned.1.call-start = ((), (), s32[]{:S(2)}) async-start(), calls=%async_computation.9 | async-start | bytes 557056 | tf_op jit(solution)/shard_map/reduce_scatter | solution.py:281
Sparse Core Ops, SparseCore 0:
  110.3 53.4 reduce-scatter.4
  167.4 55.1 reduce-scatter.6
  226.2 55.1 reduce-scatter.8
  284.7 55.1 reduce-scatter.10
where the time goes:
time: 358 us; the launch traced here: 357 us
  waiting for transfers between devices  194 us (54%)
  blocking collectives  68.6 us (19%)
  Pallas kernels  38.3 us (11%)
  local copies, waits for them, and re-layouts  21.2 us (6%)
  between operations  13.6 us (4%)
  other arithmetic  11.8 us (3%)
  starting transfers between devices  8.81 us (2%)
    reduce_scatter x4, waiting for transfers between devices, per_device(): lax.psum_scatter(part, 'tm', scatter_dimension=0, tiled=True)[0]  194 us
    psum x1, blocking collectives, per_device(): counts = lax.psum(counts.astype(jnp.bfloat16), 'tm').astype(jnp.float32)  61.6 us
    pallas_call x4, Pallas kernels, correlate(): pl.pallas_call(correlate_kernel, grid=(periods, QUARTERS), in_specs=[pl.B...  36.2 us
    dynamic_slice x1, local copies, waits for them, and re-layouts, per_device(): piece = lax.dynamic_slice_in_dim(spectra, target * mine + i, 1, axis=1)  7.88 us
  transfers between devices with their start and end apart: 9, of which 4 were waited for; matrix products, arithmetic and copies ran while one was open for 8% of the time, Pallas kernels for 10%

commit v1 on v0

v1 whole, which is shorter than its diff:
```python
import functools
import math

import jax
import jax.numpy as jnp
import numpy as np
from jax import lax
from jax.experimental import pallas as pl
from jax.experimental.pallas import tpu as pltpu
from jax.sharding import PartitionSpec as P

LAGS = 256
QUARTERS = 4
LANES = 128
SUB = 8
TILE = 4
MESH = pl.DeviceIdType.MESH


def lag_tables(channels):
    lags = np.arange(1, LAGS // 2 + 1)
    j = np.arange(channels // QUARTERS)
    angle = (j[:, None] * lags[None, :] % channels) * (2.0 * np.pi / channels)
    table = np.concatenate([np.cos(angle), np.sin(angle)], axis=1).astype(np.float32)
    high = table.astype(jnp.bfloat16)
    low = (table - high.astype(np.float32)).astype(jnp.bfloat16)
    return high, low


def pair_rows(stations):
    tiles = stations // TILE
    off = [(x * TILE, y * TILE) for x in range(tiles) for y in range(x + 1, tiles)]
    real, imag = {}, {}
    for x, y in off:
        for i in range(TILE):
            for j in range(TILE):
                real[x + i, y + j] = len(real)
    for x in range(tiles):
        for i in range(TILE):
            for j in range(i, TILE):
                real[x * TILE + i, x * TILE + j] = len(real)
    top = len(real)
    for x, y in off:
        for i in range(TILE):
            for j in range(TILE):
                imag[x + i, y + j] = top + len(imag)
    for x in range(tiles):
        for i in range(TILE):
            for j in range(i + 1, TILE):
                imag[x * TILE + i, x * TILE + j] = top + len(imag)
    return off, real, imag


def pick_matrix(stations, groups, owners):
    _, real, imag = pair_rows(stations)
    split = owners // stations
    wide = groups * split
    local = stations // groups
    span = stations // split
    pick = np.zeros((owners, 2, span, stations * stations), np.float32)
    for t in range(owners):
        a = t % wide // split * local + t // wide
        for n in range(span):
            b = t % split * span + n
            key = (min(a, b), max(a, b))
            pick[t, 0, n, real[key]] = 1.0
            if a != b:
                pick[t, 1, n, imag[key]] = 1.0 if a < b else -1.0
    return pick.reshape(owners * 2 * span, stations * stations).astype(jnp.bfloat16)


def period_tables(periods, rows):
    idx = np.arange(periods)
    angle = (idx[:, None] * idx[None, :] % periods) * (2.0 * np.pi / periods)
    eye = np.eye(rows)

    def table(m):
        wide = np.einsum("rp,nm->nrpm", m, eye).reshape(rows * periods, periods * rows)
        return jnp.asarray(wide.astype(np.float32))

    return table(np.cos(angle)), table(np.sin(angle))


def dot(a, b):
    return jnp.dot(a, b, preferred_element_type=jnp.float32)


SIN = [(-1) ** n * math.pi ** (2 * n + 1) / math.factorial(2 * n + 1) for n in range(6)]
COS = [(-1) ** n * math.pi ** (2 * n) / math.factorial(2 * n) for n in range(7)]


def cos_sin_turns(turns):
    frac = turns - jnp.floor(turns + 0.5)
    square = frac * frac
    s = jnp.full_like(square, SIN[-1])
    for coef in SIN[-2::-1]:
        s = s * square + coef
    s = s * frac
    c = jnp.full_like(square, COS[-1])
    for coef in COS[-2::-1]:
        c = c * square + coef
    return 1.0 - 2.0 * (s * s), 2.0 * (s * c)


def kernel(
    sizes,
    x_hbm, w_ref, d_ref, partner_ref, high_hbm, low_hbm, pick_hbm, pcos_ref, psin_ref,
    out_ref,
    xall, wbuf, dbuf, wall, wf, wrow, cnt, scale_t, wide_w, wide_s, dsplat,
    th, tl, pick, wh, wl, ct, st, tmp, yr, yi, v_ref, vh, vl, z_ref,
    zs, rb, red, fs, fr, gf,
    table_sem, own_sem, xs_sem, xr_sem, ws_sem, wr_sem, gs_sem, gr_sem, rs_sem, rr_sem, fs_sem, fr_sem,
):
    groups, owners, stations, periods, depth, blocks = sizes
    local = stations // groups
    mine = periods // groups
    split = owners // stations
    wide = groups * split
    span = stations // split
    own_rows = stations // wide
    rows = stations * stations
    steps = mine * QUARTERS
    lags = LAGS // 2
    me = lax.axis_index("stn")
    t = lax.axis_index("tm")
    home = t // wide
    place = t % wide
    plane = place // split
    part = t % split

    def own_copy(i):
        rows_i = pl.ds(pl.multiple_of((i % QUARTERS) * 2 * SUB, 2 * SUB), 2 * SUB)
        return pltpu.make_async_copy(
            x_hbm.at[:, me * mine + i // QUARTERS, :, rows_i, :],
            xall.at[pl.ds(me * local, local), i // QUARTERS, :, rows_i, :],
            own_sem.at[i],
        )

    tables = [
        pltpu.make_async_copy(high_hbm, th, table_sem.at[0]),
        pltpu.make_async_copy(low_hbm, tl, table_sem.at[1]),
        pltpu.make_async_copy(pick_hbm, pick, table_sem.at[2]),
        pltpu.make_async_copy(w_ref.at[me], wbuf.at[me], table_sem.at[3]),
        pltpu.make_async_copy(d_ref.at[me], dbuf.at[me], table_sem.at[4]),
    ]

    barrier = pltpu.get_barrier_semaphore()
    for shift in range(1, groups):
        for w in range(wide):
            peer = {"stn": lax.rem(me + shift, groups), "tm": home * wide + lax.rem(place + w, wide)}
            pl.semaphore_signal(barrier, inc=1, device_id=peer, device_id_type=MESH)
    for shift in range(1, owners):
        pl.semaphore_signal(barrier, inc=1, device_id={"tm": lax.rem(t + shift, owners)}, device_id_type=MESH)
    for copy in tables:
        copy.start()

    def start_own(i, _):
        own_copy(i).start()
        return 0

    lax.fori_loop(0, steps, start_own, 0)
    pl.semaphore_wait(barrier, (groups - 1) * wide + owners - 1)

    def small_copies(shift, source):
        target = lax.rem(me + shift, groups)
        return [
            pltpu.make_async_remote_copy(
                src_ref=ref.at[target], dst_ref=buf.at[source], send_sem=ws_sem.at[n, shift],
                recv_sem=wr_sem.at[n, source], device_id={"stn": target}, device_id_type=MESH,
            )
            for n, (ref, buf) in enumerate(((w_ref, wbuf), (d_ref, dbuf)))
        ]

    def spectra_copy(shift, source, i):
        target = lax.rem(me + shift, groups)
        rows_i = pl.ds(pl.multiple_of((i % QUARTERS) * 2 * SUB, 2 * SUB), 2 * SUB)
        return pltpu.make_async_remote_copy(
            src_ref=x_hbm.at[:, target * mine + i // QUARTERS, :, rows_i, :],
            dst_ref=xall.at[pl.ds(source * local, local), i // QUARTERS, :, rows_i, :],
            send_sem=xs_sem.at[shift, i], recv_sem=xr_sem.at[source, i],
            device_id={"stn": target}, device_id_type=MESH,
        )

    for shift in range(1, groups):
        for copy in small_copies(shift, me):
            copy.start()

    def start_spectra(i, _):
        for shift in range(1, groups):
            spectra_copy(shift, me, i).start()
        return 0

    lax.fori_loop(0, steps, start_spectra, 0)

    for copy in tables[3:]:
        copy.wait()
    for shift in range(1, groups):
        for copy in small_copies(shift, lax.rem(me + groups - shift, groups)):
            copy.wait_recv()

    def gather_copy(shift, source):
        return pltpu.make_async_remote_copy(
            src_ref=wbuf, dst_ref=wall.at[source], send_sem=gs_sem.at[shift], recv_sem=gr_sem.at[source],
            device_id={"tm": lax.rem(t + shift, owners)}, device_id_type=MESH,
        )

    for shift in range(1, owners):
        gather_copy(shift, t).start()
    wall[t] = wbuf[...]

    for copy in tables[:3]:
        copy.wait()
    lag = lax.broadcasted_iota(jnp.int32, (1, lags), 1) + 1
    for quarter in range(QUARTERS):
        turn = (lag * quarter) % 4
        cq = jnp.where(turn == 0, 1.0, jnp.where(turn == 2, -1.0, 0.0))
        sq = jnp.where(turn == 1, 1.0, jnp.where(turn == 3, -1.0, 0.0))

        def turn_rows(n, _, quarter=quarter, cq=cq, sq=sq):
            r = pl.ds(pl.multiple_of(n * LANES, LANES), LANES)
            for source, target in ((th, wh), (tl, wl)):
                c = source[r, :lags].astype(jnp.float32)
                s = source[r, lags:].astype(jnp.float32)
                target[quarter, r, :lags] = (c * cq - s * sq).astype(jnp.bfloat16)
                target[quarter, r, lags:] = (s * cq + c * sq).astype(jnp.bfloat16)
            return 0

        lax.fori_loop(0, th.shape[0] // LANES, turn_rows, 0)

    for g in range(groups):
        for l in range(local):
            wrow[(g * local + l) * depth : (g * local + l + 1) * depth, :] = wbuf[g, l].astype(jnp.float32)
        d = dbuf[g]
        for p in range(mine):
            dsplat[p, g * local * depth : (g + 1) * local * depth, :] = jnp.broadcast_to(d[:, p : p + 1], d.shape)
    w_t = wrow[...].T
    for r in range(stations * depth):
        wide_w[r] = jnp.broadcast_to(w_t[:, r : r + 1], (w_t.shape[0], LANES))

    for shift in range(1, owners):
        gather_copy(shift, lax.rem(t + owners - shift, owners)).wait_recv()

    def widen(n, _):
        for g in range(groups):
            for l in range(local):
                wf[g * local + l, n] = wall[n, g, l].astype(jnp.float32)
        return 0

    lax.fori_loop(0, owners, widen, 0)
    off, real_row, imag_row = pair_rows(stations)
    for a in range(stations):
        for b0 in range(a // TILE * TILE, stations, TILE):
            b = max(a, b0)
            count = b0 + TILE - b
            product = jnp.sum(wf[a][None] * wf[b : b + count], axis=1)
            cnt[real_row[a, b] : real_row[a, b] + count, :] = jnp.sum(product, axis=1)
    pairs = len(real_row)
    pad = cnt.shape[0]
    scale_t[...] = (1.0 / jnp.sqrt(jnp.maximum(cnt[...], 1.0))).T
    for m in range(pairs):
        wide_s[m] = jnp.broadcast_to(scale_t[:, m : m + 1], (scale_t.shape[0], LANES))

    channel = (
        lax.broadcasted_iota(jnp.int32, (SUB, LANES), 0) * LANES + lax.broadcasted_iota(jnp.int32, (SUB, LANES), 1)
    ).astype(jnp.float32)
    v_flat = v_ref.reshape(rows * SUB, LANES)

    def scatter_copy(p, shift, target, source):
        return pltpu.make_async_remote_copy(
            src_ref=zs.at[p, target], dst_ref=rb.at[p, source], send_sem=rs_sem.at[p, shift],
            recv_sem=rr_sem.at[p, source], device_id={"tm": lax.rem(t + shift, owners)}, device_id_type=MESH,
        )

    def final_copy(p, w, source, piece):
        return pltpu.make_async_remote_copy(
            src_ref=fs.at[p, w], dst_ref=fr.at[source, piece, p], send_sem=fs_sem.at[p, w],
            recv_sem=fr_sem.at[source, piece, p], device_id={"stn": plane, "tm": home * wide + w}, device_id_type=MESH,
        )

    def reduce_period(p):
        total = zs[p, t].astype(jnp.float32)
        for shift in range(1, owners):
            source = lax.rem(t + owners - shift, owners)
            scatter_copy(p, shift, t, source).wait_recv()
        for shift in range(1, owners):
            total = total + rb[p, lax.rem(t + owners - shift, owners)].astype(jnp.float32)
        red[...] = total.reshape(red.shape)
        for w in range(wide):
            for n in range(own_rows):
                b = partner_ref[w * own_rows + n]
                if split > 1:
                    keep = jnp.where(b // span == part, 1.0, 0.0)
                    b = b % span
                for ri in range(2):
                    row = red[ri, pl.ds(b, 1), :]
                    fs[p, w, ri, n : n + 1, :] = row * keep if split > 1 else row
        for w in range(wide):
            to_self = (plane == me) & (w == place)

            @pl.when(to_self)
            def _():
                fr[me, part, p] = fs[p, w]

            @pl.when(jnp.logical_not(to_self))
            def _():
                final_copy(p, w, me, part).start()

    def step(i, _):
        p = i // QUARTERS
        quarter = i % QUARTERS
        at = pl.ds(pl.multiple_of(p * blocks + quarter * SUB, SUB), SUB)
        index = channel + (quarter * (SUB * LANES)).astype(jnp.float32)

        def turn_tables(r, _):
            c, s = cos_sin_turns(dsplat[p, pl.ds(r, 1), :] * index)
            w = wide_w[r, at, :]
            ct[r] = c * w
            st[r] = s * w
            return 0

        lax.fori_loop(0, stations * depth, turn_tables, 0, unroll=4)

        own_copy(i).wait()
        for shift in range(1, groups):
            spectra_copy(shift, lax.rem(me + groups - shift, groups), i).wait_recv()

        rows_i = pl.ds(pl.multiple_of(quarter * 2 * SUB, 2 * SUB), 2 * SUB)

        def rotate(s, _):
            for k in range(depth):
                tmp[k] = xall[s, p, k, rows_i, :].astype(jnp.float32)
                real = tmp[k, pl.ds(0, SUB, stride=2), :]
                imag = tmp[k, pl.ds(1, SUB, stride=2), :]
                c = ct[s * depth + k]
                sn = st[s * depth + k]
                yr[k, s] = (real * c + imag * sn).astype(jnp.bfloat16).astype(jnp.float32)
                yi[k, s] = (imag * c - real * sn).astype(jnp.bfloat16).astype(jnp.float32)
            return 0

        lax.fori_loop(0, stations, rotate, 0)

        for x, y in off:
            real = None
            for k in range(depth):
                ar, ai = yr[k, x : x + TILE][:, None], yi[k, x : x + TILE][:, None]
                br, bi = yr[k, y : y + TILE][None], yi[k, y : y + TILE][None]
                re = ar * br + ai * bi
                im = ai * br - ar * bi
                real = re if real is None else real + re
                imag = im if k == 0 else imag + im
            n = TILE * TILE
            m = real_row[x, y]
            q = imag_row[x, y]
            scale = wide_s[m : m + n, at, :]
            v_ref[m : m + n] = real.reshape(n, SUB, LANES) * scale
            v_ref[q : q + n] = imag.reshape(n, SUB, LANES) * scale
        for x in range(0, stations, TILE):
            for i0 in range(TILE):
                n = TILE - i0
                a = x + i0
                for k in range(depth):
                    ar, ai = yr[k, a : a + 1], yi[k, a : a + 1]
                    br, bi = yr[k, a : a + n], yi[k, a : a + n]
                    re = ar * br + ai * bi
                    real = re if k == 0 else real + re
                    if n > 1:
                        im = ai * br[1:] - ar * bi[1:]
                        imag = im if k == 0 else imag + im
                m = real_row[a, a]
                scale = wide_s[m : m + n, at, :]
                v_ref[m : m + n] = real * scale
                if n > 1:
                    q = imag_row[a, a + 1]
                    v_ref[q : q + n - 1] = imag * scale[1:]

        for b in range(SUB):
            v = v_flat[pl.ds(b, rows, stride=SUB), :]
            high = v.astype(jnp.bfloat16)
            cols = slice(b * LANES, (b + 1) * LANES)
            vh[:, cols] = high
            vl[:, cols] = (v - high.astype(jnp.float32)).astype(jnp.bfloat16)
        values = dot(vh[...], wh[quarter]) + dot(vh[...], wl[quarter]) + dot(vl[...], wh[quarter])

        @pl.when(quarter == 0)
        def _():
            z_ref[...] = values

        @pl.when(quarter > 0)
        def _():
            z_ref[...] += values

        @pl.when(quarter == QUARTERS - 1)
        def _():
            picked = dot(pick[...], z_ref[...].astype(jnp.bfloat16)).astype(jnp.bfloat16)
            zs[p] = picked.reshape(zs.shape[1:])
            for shift in range(1, owners):
                scatter_copy(p, shift, lax.rem(t + shift, owners), t).start()

        @pl.when((quarter == QUARTERS - 1) & (p > 0))
        def _():
            reduce_period(p - 1)

        return 0

    lax.fori_loop(0, steps, step, 0)
    reduce_period(mine - 1)

    for p in range(mine):
        for g in range(groups):
            for h in range(split):
                from_self = (me == g) & (place == me * split + h)

                @pl.when(jnp.logical_not(from_self))
                def _():
                    final_copy(p, 0, g, h).wait_recv()

    for g in range(groups):
        for p in range(mine):
            value = fr[g, 0, p]
            for h in range(1, split):
                value = value + fr[g, h, p]
            r = (g * mine + p) * own_rows
            gf[:, r : r + own_rows, :] = value

    highest = lax.Precision.HIGHEST
    rc, rs = gf[0, :, :lags], gf[0, :, lags:]
    ic, im_s = gf[1, :, :lags], gf[1, :, lags:]
    flip = (
        lax.broadcasted_iota(jnp.int32, (lags, lags), 0) + lax.broadcasted_iota(jnp.int32, (lags, lags), 1) == lags - 1
    ).astype(jnp.float32)
    pcos = pcos_ref[...]
    psin = psin_ref[...]
    factor = 1.0 / math.sqrt(periods * blocks * LANES)

    def mix(m, v):
        return jnp.dot(m, v, precision=highest, preferred_element_type=jnp.float32)

    for side in range(2):
        if side == 0:
            real, imag = mix(rc - im_s, flip), mix(ic + rs, flip)
        else:
            real, imag = rc + im_s, ic - rs
        cols = slice(side * lags, (side + 1) * lags)
        out_ref[0, :, cols] = (mix(pcos, real) + mix(psin, imag)) * factor
        out_ref[1, :, cols] = (mix(pcos, imag) - mix(psin, real)) * factor

    for shift in range(1, groups):
        for copy in small_copies(shift, me):
            copy.wait_send()
    for shift in range(1, owners):
        gather_copy(shift, t).wait_send()

    def sent(i, _):
        for shift in range(1, groups):
            spectra_copy(shift, me, i).wait_send()
        return 0

    lax.fori_loop(0, steps, sent, 0)

    def scattered(p, _):
        for shift in range(1, owners):
            scatter_copy(p, shift, lax.rem(t + shift, owners), t).wait_send()
        for w in range(wide):
            @pl.when(jnp.logical_not((plane == me) & (w == place)))
            def _():
                final_copy(p, w, me, part).wait_send()
        return 0

    lax.fori_loop(0, mine, scattered, 0)


def per_device(spectra, flags, poly_index, delay_model, partner_order):
    local, periods, depth, _, channels = spectra.shape
    groups = lax.axis_size("stn")
    owners = lax.axis_size("tm")
    me = lax.axis_index("stn")
    stations = local * groups
    mine = periods // groups
    blocks = flags.shape[-1]
    split = owners // stations
    wide = groups * split
    own_rows = stations // wide
    span = stations // split
    rows = stations * stations
    steps = mine * QUARTERS
    width = channels // QUARTERS
    assert channels == blocks * LANES and width == SUB * LANES and stations % TILE == 0

    x = spectra.reshape(local, periods, depth, 2, blocks, LANES).transpose(0, 1, 2, 4, 3, 5)
    x = x.reshape(local, periods, depth, 2 * blocks, LANES)

    lanes = -(-mine * blocks // LANES) * LANES
    w = (1.0 - flags.astype(jnp.float32)).astype(jnp.bfloat16)
    w = w.reshape(local, groups, mine, depth, blocks).transpose(1, 0, 3, 2, 4).reshape(groups, local, depth, mine * blocks)
    w = jnp.pad(w, ((0, 0), (0, 0), (0, 0), (0, lanes - mine * blocks)))

    total = depth * owners
    times = (
        jnp.arange(periods, dtype=jnp.int32)[:, None] * total
        + lax.axis_index("tm") * depth
        + jnp.arange(depth, dtype=jnp.int32)[None, :]
    ).astype(jnp.float32)
    moment = times / float(periods * total)
    table_rows = delay_model.shape[0]
    onehot = poly_index[..., None] == jnp.arange(table_rows, dtype=jnp.int32)
    coef = [jnp.sum(jnp.where(onehot, delay_model[:, n], 0.0), axis=-1) for n in range(3)]
    delay = (coef[0] + coef[1] * moment + coef[2] * moment * moment) * (0.5 / channels)
    d = delay.reshape(local, groups, mine, depth).transpose(1, 0, 3, 2).reshape(groups, local * depth, mine)
    d = jnp.pad(d, ((0, 0), (0, 0), (0, LANES - mine)))

    high, low = lag_tables(channels)
    pick = pick_matrix(stations, groups, owners)
    pcos, psin = period_tables(periods, own_rows)
    any_spec = pl.BlockSpec(memory_space=pl.ANY)
    vmem = pl.BlockSpec(memory_space=pltpu.VMEM)
    f32, bf16 = jnp.float32, jnp.bfloat16
    pad = -(-rows // LANES) * LANES
    dma = pltpu.SemaphoreType.DMA
    out = pl.pallas_call(
        functools.partial(kernel, (groups, owners, stations, periods, depth, blocks)),
        out_shape=jax.ShapeDtypeStruct((2, own_rows * periods, LAGS), f32),
        in_specs=[any_spec, vmem, vmem, pl.BlockSpec(memory_space=pltpu.SMEM), any_spec, any_spec, any_spec, vmem, vmem],
        out_specs=vmem,
        scratch_shapes=[
            pltpu.VMEM((stations, mine, depth, 2 * blocks, LANES), bf16),
            pltpu.VMEM((groups, local, depth, lanes), bf16),
            pltpu.VMEM((groups, local * depth, LANES), f32),
            pltpu.VMEM((owners, groups, local, depth, lanes), bf16),
            pltpu.VMEM((stations, owners, depth, lanes), f32),
            pltpu.VMEM((stations * depth, lanes), f32),
            pltpu.VMEM((pad, lanes), f32),
            pltpu.VMEM((lanes, pad), f32),
            pltpu.VMEM((stations * depth, lanes, LANES), f32),
            pltpu.VMEM((stations * (stations + 1) // 2, lanes, LANES), f32),
            pltpu.VMEM((mine, stations * depth, LANES), f32),
            pltpu.VMEM(high.shape, bf16),
            pltpu.VMEM(low.shape, bf16),
            pltpu.VMEM(pick.shape, bf16),
            pltpu.VMEM((QUARTERS,) + high.shape, bf16),
            pltpu.VMEM((QUARTERS,) + low.shape, bf16),
            pltpu.VMEM((stations * depth, SUB, LANES), f32),
            pltpu.VMEM((stations * depth, SUB, LANES), f32),
            pltpu.VMEM((depth, 2 * SUB, LANES), f32),
            pltpu.VMEM((depth, stations, SUB, LANES), f32),
            pltpu.VMEM((depth, stations, SUB, LANES), f32),
            pltpu.VMEM((rows, SUB, LANES), f32),
            pltpu.VMEM((rows, width), bf16),
            pltpu.VMEM((rows, width), bf16),
            pltpu.VMEM((rows, LAGS), f32),
            pltpu.VMEM((mine, owners, 2 * span, LAGS), bf16),
            pltpu.VMEM((mine, owners, 2 * span, LAGS), bf16),
            pltpu.VMEM((2, span, LAGS), f32),
            pltpu.VMEM((mine, wide, 2, own_rows, LAGS), f32),
            pltpu.VMEM((groups, split, mine, 2, own_rows, LAGS), f32),
            pltpu.VMEM((2, periods * own_rows, LAGS), f32),
            dma((5,)),
            dma((steps,)),
            dma((groups, steps)),
            dma((groups, steps)),
            dma((2, groups)),
            dma((2, groups)),
            dma((owners,)),
            dma((owners,)),
            dma((mine, owners)),
            dma((mine, owners)),
            dma((mine, wide)),
            dma((groups, split, mine)),
        ],
        compiler_params=pltpu.CompilerParams(collective_id=0, has_side_effects=True, vmem_limit_bytes=60 << 20),
        name="correlate",
    )(x, w, d, partner_order, jnp.asarray(high), jnp.asarray(low), jnp.asarray(pick), pcos, psin)
    return out.reshape(2, own_rows, periods, LAGS)


def solution(mesh):
    return jax.shard_map(
        per_device,
        mesh=mesh,
        in_specs=(
            P("stn", None, "tm", None, None),
            P("stn", None, "tm", None),
            P("stn", None, "tm"),
            P(),
            P(),
        ),
        out_specs=P(None, ("stn", "tm"), None, None),
        check_vma=False,
    )
```

time: 358 us -> 74.7 us (0.21)
  waiting for transfers between devices: 194 us -> 0 us
  blocking collectives: 68.6 us -> 0 us
  Pallas kernels: 38.3 us -> 68.2 us
  local copies, waits for them, and re-layouts: 21.2 us -> 4.07 us
  between operations: 13.6 us -> 0.04 us
  other arithmetic: 11.8 us -> 2.02 us
  starting transfers between devices: 8.81 us -> 0 us
    reduce_scatter x4 -> x0, waiting for transfers between devices: 194 us -> none  [per_device(): lax.psum_scatter(part, 'tm', scatter_dimension=0, tiled=True)[0]]
    psum x1 -> x0, blocking collectives: 61.6 us -> none  [per_device(): counts = lax.psum(counts.astype(jnp.bfloat16), 'tm').astype(jnp.float32)]
    pallas_call x5 -> x1, Pallas kernels: 38.3 us -> 68.2 us  [per_device(): pl.pallas_call(functools.partial(kernel, (groups, owners, stations, perio...]
    dynamic_slice x1 -> x0, local copies, waits for them, and re-layouts: 7.88 us -> none  [per_device(): piece = lax.dynamic_slice_in_dim(spectra, target * mine + i, 1, axis=1)]
    all_to_all x1 -> x0, blocking collectives: 6.98 us -> none  [per_device(): own = lax.all_to_all(own, 'stn', split_axis=1, concat_axis=0, tiled=True)]
    transpose x6 -> x1, other arithmetic: 6.5 us -> 0.08 us  [per_device(): delay.reshape(local, groups, mine, depth).transpose(1, 0, 3, 2)]
    unnamed x27 -> x1, local copies, waits for them, and re-layouts: 6.21 us -> 1.57 us
    ppermute x4 -> x0, starting transfers between devices: 4.27 us -> none  [per_device(): lax.ppermute(piece, 'stn', [(g, (g + shift) % groups) for g in range(grou...]
  transfers between devices with their start and end apart: 9 -> 0, of which waited for: 4 -> 0; matrix products, arithmetic and copies ran while one was open for 8% -> 0% of each run, Pallas kernels for 10% -> 0%
where the time goes in v1:
time: 74.7 us; the launch traced here: 74.4 us
  Pallas kernels  68.2 us (91%)
  local copies, waits for them, and re-layouts  4.07 us (5%)
  other arithmetic  2.02 us (3%)
    pallas_call x1, Pallas kernels, per_device(): pl.pallas_call(functools.partial(kernel, (groups, owners, stations, perio...  68.2 us
    unnamed x1, local copies, waits for them, and re-layouts  1.57 us

profile of v1, /device:TPU:0, one launch (start us, length us, event | category | flops | bytes accessed | tf_op | source)
XLA Modules:
  0.0 74.4 jit_solution(8188076601779994767)
XLA Ops:
  0.0 0.8 %slice_bitcast_fusion.2 = (f32[64]{0:T(128)S(1)}, f32[64]{0:T(128)S(1)}, f32[64]{0:T(128)S(1)}) fusion(f32[64,3]{0,1:T(4,128)} %param.13), kind=kLoop, calls=%fused_computation.11 | loop fusion | bytes 1536 | tf_op jit(solution)/shard_map/squeeze | solution.py:506
  0.8 1.0 %select_reduce_fusion.1 = (f32[8,8,4]{1,2,0:T(4,128)S(1)}, f32[8,8,4]{1,2,0:T(4,128)S(1)}, f32[8,8,4]{1,2,0:T(4,128)S(1)}) fusion(f32[64]{0:T(128)S(1)} %get-tuple-element.10, s32[8,8,4]{1,2,0:T(4,128)} %param.12, f32[64]{0:T(128)S(1)} %get-tuple-element.9, f32[64]{0:T(128)S(1)} %get-tuple-element.8), kind=kLoop, calls=%fused_computation.1 | loop fusion | flops 113920 | bytes 4864 | tf_op jit(solution)/shard_map/reduce_sum | solution.py:506
  1.8 0.1 copy.21
  1.9 0.1 copy.22
  2.0 0.1 copy.20
  2.0 0.1 multiply_bitcast_fusion
  2.1 0.1 copy.23
  2.3 0.6 pad.4.d_ref
  2.9 0.9 %subtract_convert_fusion = bf16[8,8,4,32]{3,2,1,0:T(4,128)(2,1)S(1)} fusion(s32[8,8,4,32]{3,2,1,0:T(4,128)} %param.11), kind=kLoop, calls=%fused_computation.4 | loop fusion | flops 24576 | bytes 49152 | tf_op jit(solution)/shard_map/convert_element_type | solution.py:493
  3.9 0.7 reshape.61.w_ref
  4.6 68.2 %correlate.1 = f32[2,64,256]{2,1,0:T(8,128)} custom-call(bf16[8,8,4,64,128]{4,3,2,1,0:T(8,128)(2,1)} %bitcast.22, bf16[2,8,4,128]{3,2,1,0:T(4,128)(2,1)} %reshape.61.w_ref, f32[2,32,128]{2,1,0:T(8,128)} %pad.4.d_ref, s32[16]{0:T(128)} %partner_ref.1, bf16[1024,256]{1,0:T(8,128)(2,1)} %constant.32.clone.high_hbm, bf16[1024,256]{1,0:T(8,128)(2,1)} %constant.33.clone.low_hbm, ...), custom_call_target="tpu_custom_call" | custom-call | tf_op jit(solution)/shard_map/correlate/pallas_call | solution.py:519
  72.8 1.6 %copy.27 = f32[2,8,8,256]{3,2,1,0:T(8,128)} copy(f32[2,8,8,256]{3,2,1,0:T(8,128)} %bitcast.23) | data formatting | bytes 262144
  (3 shorter events, 0.0 us)

commit v2 on v1

v2 whole, which is shorter than its diff:
```python
import functools
import math

import jax
import jax.numpy as jnp
import numpy as np
from jax import lax
from jax.experimental import pallas as pl
from jax.experimental.pallas import tpu as pltpu
from jax.sharding import PartitionSpec as P

LAGS = 256
QUARTERS = 4
LANES = 128
SUB = 8
TILE = 4
MESH = pl.DeviceIdType.MESH


def lag_tables(channels):
    lags = np.arange(1, LAGS // 2 + 1)
    j = np.arange(channels // QUARTERS)
    angle = (j[:, None] * lags[None, :] % channels) * (2.0 * np.pi / channels)
    table = np.concatenate([np.cos(angle), np.sin(angle)], axis=1).astype(np.float32)
    high = table.astype(jnp.bfloat16)
    low = (table - high.astype(np.float32)).astype(jnp.bfloat16)
    return high, low


def pair_rows(stations):
    tiles = stations // TILE
    off = [(x * TILE, y * TILE) for x in range(tiles) for y in range(x + 1, tiles)]
    real, imag = {}, {}
    for x, y in off:
        for i in range(TILE):
            for j in range(TILE):
                real[x + i, y + j] = len(real)
    for x in range(tiles):
        for i in range(TILE):
            for j in range(i, TILE):
                real[x * TILE + i, x * TILE + j] = len(real)
    top = len(real)
    for x, y in off:
        for i in range(TILE):
            for j in range(TILE):
                imag[x + i, y + j] = top + len(imag)
    for x in range(tiles):
        for i in range(TILE):
            for j in range(i + 1, TILE):
                imag[x * TILE + i, x * TILE + j] = top + len(imag)
    return off, real, imag


def pick_matrix(stations, groups, owners):
    _, real, imag = pair_rows(stations)
    split = owners // stations
    wide = groups * split
    local = stations // groups
    span = stations // split
    pick = np.zeros((groups, owners, 2, span, stations * stations), np.float32)
    for g in range(groups):
        for t in range(owners):
            a = (t % wide // split * local + t // wide - g * local) % stations
            for n in range(span):
                b = (t % split * span + n - g * local) % stations
                key = (min(a, b), max(a, b))
                pick[g, t, 0, n, real[key]] = 1.0
                if a != b:
                    pick[g, t, 1, n, imag[key]] = 1.0 if a < b else -1.0
    return pick.reshape(groups, owners * 2 * span, stations * stations).astype(jnp.bfloat16)


def period_tables(periods, rows):
    idx = np.arange(periods)
    angle = (idx[:, None] * idx[None, :] % periods) * (2.0 * np.pi / periods)
    eye = np.eye(rows)

    def table(m):
        wide = np.einsum("rp,nm->nrpm", m, eye).reshape(rows * periods, periods * rows)
        return jnp.asarray(wide.astype(np.float32))

    return table(np.cos(angle)), table(np.sin(angle))


def dot(a, b):
    return jnp.dot(a, b, preferred_element_type=jnp.float32)


SIN = [(-1) ** n * math.pi ** (2 * n + 1) / math.factorial(2 * n + 1) for n in range(6)]
COS = [(-1) ** n * math.pi ** (2 * n) / math.factorial(2 * n) for n in range(7)]


def cos_sin_turns(turns):
    frac = turns - jnp.floor(turns + 0.5)
    square = frac * frac
    s = jnp.full_like(square, SIN[-1])
    for coef in SIN[-2::-1]:
        s = s * square + coef
    s = s * frac
    c = jnp.full_like(square, COS[-1])
    for coef in COS[-2::-1]:
        c = c * square + coef
    return 1.0 - 2.0 * (s * s), 2.0 * (s * c)


def kernel(
    sizes,
    x_hbm, flags_hbm, index_hbm, model_ref, partner_ref, high_hbm, low_hbm, pick_hbm, pcos_hbm, psin_hbm,
    out_ref,
    xall, flags, index_ref, pcos_ref, psin_ref, wsend, dsend, wbuf, dbuf, wall, wf, wrow, acc, scale_ref, turned,
    wide_w, dsplat, step_c, step_s, base_c, base_s, th, tl, pick, wh, wl, tmp, yr, yi, ys, yd, v_ref, vh, z_ref,
    zs, rb, red, fs, fr, gf,
    table_sem, own_sem, xs_sem, xr_sem, ws_sem, wr_sem, gs_sem, gr_sem, rs_sem, rr_sem, fs_sem, fr_sem,
):
    groups, owners, stations, periods, depth, blocks = sizes
    local = stations // groups
    mine = periods // groups
    split = owners // stations
    wide = groups * split
    span = stations // split
    own_rows = stations // wide
    rows = stations * stations
    steps = mine * QUARTERS
    lags = LAGS // 2
    me = lax.axis_index("stn")
    t = lax.axis_index("tm")
    home = t // wide
    place = t % wide
    plane = place // split
    part = t % split

    def band(i):
        return pl.ds(pl.multiple_of((i % QUARTERS) * 2 * SUB, 2 * SUB), 2 * SUB)

    def own_copy(i):
        return pltpu.make_async_copy(
            x_hbm.at[:, me * mine + i // QUARTERS, :, band(i), :],
            xall.at[pl.ds(0, local), i // QUARTERS, :, band(i), :],
            own_sem.at[i],
        )

    tables = [
        pltpu.make_async_copy(source, target, table_sem.at[n])
        for n, (source, target) in enumerate((
            (flags_hbm, flags), (index_hbm, index_ref), (high_hbm, th), (low_hbm, tl), (pick_hbm.at[me], pick),
            (pcos_hbm, pcos_ref), (psin_hbm, psin_ref),
        ))
    ]
    barrier = pltpu.get_barrier_semaphore()
    for shift in range(1, groups):
        for w in range(wide):
            peer = {"stn": lax.rem(me + shift, groups), "tm": home * wide + lax.rem(place + w, wide)}
            pl.semaphore_signal(barrier, inc=1, device_id=peer, device_id_type=MESH)
    for shift in range(1, owners):
        pl.semaphore_signal(barrier, inc=1, device_id={"tm": lax.rem(t + shift, owners)}, device_id_type=MESH)
    for copy in tables:
        copy.start()

    def start_own(i, _):
        own_copy(i).start()
        return 0

    lax.fori_loop(0, steps, start_own, 0)

    tables[1].wait()
    index = index_ref[...]

    def look_up(n, coef):
        here = index == n
        return tuple(jnp.where(here, model_ref[c, n], coef[c]) for c in range(3))

    none = jnp.zeros(index.shape, jnp.float32)
    coef = lax.fori_loop(0, model_ref.shape[1], look_up, (none, none, none), unroll=4)
    total = depth * owners
    times = (
        lax.broadcasted_iota(jnp.int32, index.shape, 2) * total + t * depth + lax.broadcasted_iota(jnp.int32, index.shape, 1)
    ).astype(jnp.float32)
    moment = times / float(periods * total)
    delay = (coef[0] + coef[1] * moment + coef[2] * moment * moment) * (0.5 / (blocks * LANES))
    dsend[...] = jnp.zeros_like(dsend)
    for g in range(groups):
        dsend[g, :, :, :mine] = delay[:, :, g * mine : (g + 1) * mine]
    tables[0].wait()
    for g in range(groups):
        pieces = [flags[:, g * mine + p].astype(jnp.float32) for p in range(mine)]
        gap = wsend.shape[-1] - mine * blocks
        if gap:
            pieces.append(jnp.ones(pieces[0].shape[:-1] + (gap,), jnp.float32))
        both = jnp.concatenate(pieces, axis=-1) if len(pieces) > 1 else pieces[0]
        wsend[g] = (1.0 - both).astype(jnp.bfloat16)
    wbuf[0] = wsend[me]
    dbuf[0] = dsend[me]
    pl.semaphore_wait(barrier, (groups - 1) * wide + owners - 1)

    def small_copies(shift):
        target = lax.rem(me + shift, groups)
        return [
            pltpu.make_async_remote_copy(
                src_ref=ref.at[target], dst_ref=buf.at[groups - shift], send_sem=ws_sem.at[n, shift],
                recv_sem=wr_sem.at[n, shift], device_id={"stn": target}, device_id_type=MESH,
            )
            for n, (ref, buf) in enumerate(((wsend, wbuf), (dsend, dbuf)))
        ]

    def spectra_copy(shift, i):
        target = lax.rem(me + shift, groups)
        return pltpu.make_async_remote_copy(
            src_ref=x_hbm.at[:, target * mine + i // QUARTERS, :, band(i), :],
            dst_ref=xall.at[pl.ds((groups - shift) * local, local), i // QUARTERS, :, band(i), :],
            send_sem=xs_sem.at[shift, i], recv_sem=xr_sem.at[shift, i],
            device_id={"stn": target}, device_id_type=MESH,
        )

    for shift in range(1, groups):
        for copy in small_copies(shift):
            copy.start()

    def start_spectra(i, _):
        for shift in range(1, groups):
            spectra_copy(shift, i).start()
        return 0

    lax.fori_loop(0, steps, start_spectra, 0)

    for copy in tables[2:]:
        copy.wait()
    lag = lax.broadcasted_iota(jnp.int32, (1, lags), 1) + 1
    for quarter in range(QUARTERS):
        turn = (lag * quarter) % 4
        cq = jnp.where(turn == 0, 1.0, jnp.where(turn == 2, -1.0, 0.0))
        sq = jnp.where(turn == 1, 1.0, jnp.where(turn == 3, -1.0, 0.0))

        def turn_rows(n, _, quarter=quarter, cq=cq, sq=sq):
            r = pl.ds(pl.multiple_of(n * LANES, LANES), LANES)
            for source, target in ((th, wh), (tl, wl)):
                c = source[r, :lags].astype(jnp.float32)
                s = source[r, lags:].astype(jnp.float32)
                target[quarter, r, :lags] = (c * cq - s * sq).astype(jnp.bfloat16)
                target[quarter, r, lags:] = (s * cq + c * sq).astype(jnp.bfloat16)
            return 0

        lax.fori_loop(0, th.shape[0] // LANES, turn_rows, 0)

    for shift in range(1, groups):
        for copy in small_copies(shift):
            copy.wait_recv()

    def gather_copy(shift, source):
        return pltpu.make_async_remote_copy(
            src_ref=wbuf, dst_ref=wall.at[source], send_sem=gs_sem.at[shift], recv_sem=gr_sem.at[source],
            device_id={"tm": lax.rem(t + shift, owners)}, device_id_type=MESH,
        )

    for shift in range(1, owners):
        gather_copy(shift, t).start()
    wall[t] = wbuf[...]

    for g in range(groups):
        for l in range(local):
            r = (g * local + l) * depth
            wrow[r : r + depth, :] = wbuf[g, l].astype(jnp.float32)
            d = dbuf[g, l]
            for p in range(mine):
                dsplat[p, r : r + depth, :] = jnp.broadcast_to(d[:, p : p + 1], d.shape)
    c, s = cos_sin_turns(dsplat[...] * float(SUB * LANES))
    step_c[...] = c
    step_s[...] = s
    channel = (
        lax.broadcasted_iota(jnp.int32, (SUB, LANES), 0) * LANES + lax.broadcasted_iota(jnp.int32, (SUB, LANES), 1)
    ).astype(jnp.float32)
    spectra = stations * depth

    def start_phase(n, _):
        p = n // spectra
        r = n % spectra
        c, s = cos_sin_turns(dsplat[p, pl.ds(r, 1), :] * channel)
        base_c[p, r] = c
        base_s[p, r] = s
        return 0

    lax.fori_loop(0, mine * spectra, start_phase, 0, unroll=8)
    w_t = wrow[...].T
    for r in range(spectra):
        wide_w[r] = jnp.broadcast_to(w_t[:, r : r + 1], (w_t.shape[0], LANES))

    off, real_row, imag_row = pair_rows(stations)
    pairs = len(real_row)
    acc_flat = acc.reshape(pairs * SUB, LANES)
    v_flat = v_ref.reshape(rows * SUB, LANES)

    def make_scale():
        for shift in range(1, owners):
            gather_copy(shift, lax.rem(t + owners - shift, owners)).wait_recv()
        for n in range(owners):
            wf[:, n * depth : (n + 1) * depth, :] = wall[n].astype(jnp.float32).reshape(stations, depth, LANES)
        for a in range(stations):
            for b0 in range(a // TILE * TILE, stations, TILE):
                b = max(a, b0)
                count = b0 + TILE - b
                product = wf[a][None] * wf[b : b + count]
                m = real_row[a, b]
                acc[m : m + count] = jnp.sum(product.reshape(count, owners * depth // SUB, SUB, LANES), axis=1)
        count = acc_flat[pl.ds(0, pairs, stride=SUB), :]
        for b in range(1, SUB):
            count = count + acc_flat[pl.ds(b, pairs, stride=SUB), :]
        scale_ref[:pairs, :] = 1.0 / jnp.sqrt(jnp.maximum(count, 1.0))
        n = len(off) * TILE * TILE
        if n:
            scale_ref[pairs : pairs + n, :] = scale_ref[:n, :]
        for x in range(0, stations, TILE):
            for i in range(TILE - 1):
                m, q, n = real_row[x + i, x + i + 1], imag_row[x + i, x + i + 1], TILE - 1 - i
                scale_ref[q : q + n, :] = scale_ref[m : m + n, :]

    def scatter_copy(p, shift, target, source):
        return pltpu.make_async_remote_copy(
            src_ref=zs.at[p, target], dst_ref=rb.at[p, source], send_sem=rs_sem.at[p, shift],
            recv_sem=rr_sem.at[p, source], device_id={"tm": lax.rem(t + shift, owners)}, device_id_type=MESH,
        )

    def final_copy(p, w, source, piece):
        return pltpu.make_async_remote_copy(
            src_ref=fs.at[p, w], dst_ref=fr.at[source, piece, p], send_sem=fs_sem.at[p, w],
            recv_sem=fr_sem.at[source, piece, p], device_id={"stn": plane, "tm": home * wide + w}, device_id_type=MESH,
        )

    def reduce_period(p):
        total = zs[p, t].astype(jnp.float32)
        for shift in range(1, owners):
            source = lax.rem(t + owners - shift, owners)
            scatter_copy(p, shift, t, source).wait_recv()
        for shift in range(1, owners):
            total = total + rb[p, lax.rem(t + owners - shift, owners)].astype(jnp.float32)
        red[...] = total.reshape(red.shape)
        for w in range(wide):
            for n in range(own_rows):
                b = partner_ref[w * own_rows + n]
                if split > 1:
                    keep = jnp.where(b // span == part, 1.0, 0.0)
                    b = b % span
                for ri in range(2):
                    row = red[ri, pl.ds(b, 1), :]
                    fs[p, w, ri, n : n + 1, :] = row * keep if split > 1 else row
        for w in range(wide):
            to_self = (plane == me) & (w == place)

            @pl.when(to_self)
            def _():
                fr[me, part, p] = fs[p, w]

            @pl.when(jnp.logical_not(to_self))
            def _():
                final_copy(p, w, me, part).start()

    def step(i, _):
        p = i // QUARTERS
        quarter = i % QUARTERS
        at = pl.ds(pl.multiple_of(p * blocks + quarter * SUB, SUB), SUB)

        own_copy(i).wait()
        for shift in range(1, groups):
            spectra_copy(shift, i).wait_recv()

        def rotate(n, _):
            for j in range(2):
                s = n * 2 + j
                for k in range(depth):
                    r = s * depth + k
                    tmp[j * depth + k] = xall[s, p, k, band(i), :].astype(jnp.float32)
                    real = tmp[j * depth + k, pl.ds(0, SUB, stride=2), :]
                    imag = tmp[j * depth + k, pl.ds(1, SUB, stride=2), :]
                    c = base_c[p, r]
                    sn = base_s[p, r]
                    w = wide_w[r, at, :]
                    new_real = (w * (real * c + imag * sn)).astype(jnp.bfloat16).astype(jnp.float32)
                    new_imag = (w * (imag * c - real * sn)).astype(jnp.bfloat16).astype(jnp.float32)
                    yr[k, s] = new_real
                    yi[k, s] = new_imag
                    ys[k, s] = new_real + new_imag
                    yd[k, s] = new_real - new_imag
                    pc = step_c[p, pl.ds(r, 1), :]
                    ps = step_s[p, pl.ds(r, 1), :]
                    base_c[p, r] = c * pc - sn * ps
                    base_s[p, r] = sn * pc + c * ps
            return 0

        lax.fori_loop(0, stations // 2, rotate, 0)

        half = TILE // 2
        for x, y0 in off:
            for y in (y0, y0 + half):
                for k in range(depth):
                    ar, ai, asum = (ref[k, x : x + TILE][:, None] for ref in (yr, yi, ys))
                    br, bi, bdiff = (ref[k, y : y + half][None] for ref in (yr, yi, yd))
                    first = ar * br if k == 0 else first + ar * br
                    second = ai * bi if k == 0 else second + ai * bi
                    third = asum * bdiff if k == 0 else third + asum * bdiff
                real = first + second
                imag = third - (first - second)
                for n in range(TILE):
                    m = real_row[x + n, y]
                    q = imag_row[x + n, y]
                    v_ref[m : m + half] = real[n]
                    v_ref[q : q + half] = imag[n]
        for x in range(0, stations, TILE):
            for a in range(x, x + TILE):
                n = x + TILE - a
                for k in range(depth):
                    ar, ai = yr[k, a], yi[k, a]
                    term = ar * ar + ai * ai
                    auto = term if k == 0 else auto + term
                    if n > 1:
                        br, bi, bdiff = yr[k, a + 1 : a + n], yi[k, a + 1 : a + n], yd[k, a + 1 : a + n]
                        asum = ys[k, a]
                        first = ar * br if k == 0 else first + ar * br
                        second = ai * bi if k == 0 else second + ai * bi
                        third = asum * bdiff if k == 0 else third + asum * bdiff
                m = real_row[a, a]
                v_ref[m] = auto
                if n > 1:
                    q = imag_row[a, a + 1]
                    v_ref[m + 1 : m + n] = first + second
                    v_ref[q : q + n - 1] = third - (first - second)

        pl.when(i == 0)(make_scale)
        turned[...] = pltpu.roll(scale_ref[...], LANES - (p * blocks + quarter * SUB), 1)
        for b in range(SUB):
            v = v_flat[pl.ds(b, rows, stride=SUB), :] * turned[:, b : b + 1]
            vh[:, b * LANES : (b + 1) * LANES] = v.astype(jnp.bfloat16)
        values = dot(vh[...], wh[quarter]) + dot(vh[...], wl[quarter])

        @pl.when(quarter == 0)
        def _():
            z_ref[...] = values

        @pl.when(quarter > 0)
        def _():
            z_ref[...] += values

        @pl.when(quarter == QUARTERS - 1)
        def _():
            picked = dot(pick[...], z_ref[...].astype(jnp.bfloat16)).astype(jnp.bfloat16)
            zs[p] = picked.reshape(zs.shape[1:])
            for shift in range(1, owners):
                scatter_copy(p, shift, lax.rem(t + shift, owners), t).start()

        @pl.when((quarter == QUARTERS - 1) & (p > 0))
        def _():
            reduce_period(p - 1)

        return 0

    lax.fori_loop(0, steps, step, 0)
    reduce_period(mine - 1)

    for p in range(mine):
        for g in range(groups):
            for h in range(split):
                from_self = (me == g) & (place == me * split + h)

                @pl.when(jnp.logical_not(from_self))
                def _():
                    final_copy(p, 0, g, h).wait_recv()

    for g in range(groups):
        for p in range(mine):
            value = fr[g, 0, p]
            for h in range(1, split):
                value = value + fr[g, h, p]
            r = (g * mine + p) * own_rows
            gf[:, r : r + own_rows, :] = value

    highest = lax.Precision.HIGHEST
    rc, rs = gf[0, :, :lags], gf[0, :, lags:]
    ic, im_s = gf[1, :, :lags], gf[1, :, lags:]
    flip = (
        lax.broadcasted_iota(jnp.int32, (lags, lags), 0) + lax.broadcasted_iota(jnp.int32, (lags, lags), 1) == lags - 1
    ).astype(jnp.float32)
    pcos = pcos_ref[...]
    psin = psin_ref[...]
    factor = 1.0 / math.sqrt(periods * blocks * LANES)

    def mix(m, v):
        return jnp.dot(m, v, precision=highest, preferred_element_type=jnp.float32)

    for side in range(2):
        if side == 0:
            real, imag = mix(rc - im_s, flip), mix(ic + rs, flip)
        else:
            real, imag = rc + im_s, ic - rs
        cols = slice(side * lags, (side + 1) * lags)
        out_ref[0, :, cols] = (mix(pcos, real) + mix(psin, imag)) * factor
        out_ref[1, :, cols] = (mix(pcos, imag) - mix(psin, real)) * factor

    for shift in range(1, groups):
        for copy in small_copies(shift):
            copy.wait_send()
    for shift in range(1, owners):
        gather_copy(shift, t).wait_send()

    def sent(i, _):
        for shift in range(1, groups):
            spectra_copy(shift, i).wait_send()
        return 0

    lax.fori_loop(0, steps, sent, 0)

    def scattered(p, _):
        for shift in range(1, owners):
            scatter_copy(p, shift, lax.rem(t + shift, owners), t).wait_send()
        for w in range(wide):
            @pl.when(jnp.logical_not((plane == me) & (w == place)))
            def _():
                final_copy(p, w, me, part).wait_send()
        return 0

    lax.fori_loop(0, mine, scattered, 0)


def per_device(spectra, flags, poly_index, delay_model, partner_order):
    local, periods, depth, _, channels = spectra.shape
    groups = lax.axis_size("stn")
    owners = lax.axis_size("tm")
    stations = local * groups
    mine = periods // groups
    blocks = flags.shape[-1]
    split = owners // stations
    wide = groups * split
    own_rows = stations // wide
    span = stations // split
    rows = stations * stations
    pairs = stations * (stations + 1) // 2
    steps = mine * QUARTERS
    width = channels // QUARTERS
    lanes = LANES
    assert channels == blocks * LANES and width == SUB * LANES and stations % TILE == 0 and mine * blocks <= lanes

    x = spectra.reshape(local, periods, depth, 2, blocks, LANES).transpose(0, 1, 2, 4, 3, 5)
    x = x.reshape(local, periods, depth, 2 * blocks, LANES)
    high, low = lag_tables(channels)
    pick = pick_matrix(stations, groups, owners)
    pcos, psin = period_tables(periods, own_rows)
    any_spec = pl.BlockSpec(memory_space=pl.ANY)
    smem = pl.BlockSpec(memory_space=pltpu.SMEM)
    f32, bf16, i32 = jnp.float32, jnp.bfloat16, jnp.int32
    spectra_rows = stations * depth
    dma = pltpu.SemaphoreType.DMA
    out = pl.pallas_call(
        functools.partial(kernel, (groups, owners, stations, periods, depth, blocks)),
        out_shape=jax.ShapeDtypeStruct((2, own_rows * periods, LAGS), f32),
        in_specs=[any_spec, any_spec, any_spec, smem, smem] + [any_spec] * 5,
        out_specs=pl.BlockSpec(memory_space=pltpu.VMEM),
        scratch_shapes=[
            pltpu.VMEM((stations, mine, depth, 2 * blocks, LANES), bf16),
            pltpu.VMEM(flags.shape, i32),
            pltpu.VMEM((local, depth, periods), i32),
            pltpu.VMEM(pcos.shape, f32),
            pltpu.VMEM(psin.shape, f32),
            pltpu.VMEM((groups, local, depth, lanes), bf16),
            pltpu.VMEM((groups, local, depth, LANES), f32),
            pltpu.VMEM((groups, local, depth, lanes), bf16),
            pltpu.VMEM((groups, local, depth, LANES), f32),
            pltpu.VMEM((owners, groups, local, depth, lanes), bf16),
            pltpu.VMEM((stations, owners * depth, lanes), f32),
            pltpu.VMEM((spectra_rows, lanes), f32),
            pltpu.VMEM((pairs, SUB, lanes), f32),
            pltpu.VMEM((rows, lanes), f32),
            pltpu.VMEM((rows, lanes), f32),
            pltpu.VMEM((spectra_rows, lanes, LANES), f32),
            pltpu.VMEM((mine, spectra_rows, LANES), f32),
            pltpu.VMEM((mine, spectra_rows, LANES), f32),
            pltpu.VMEM((mine, spectra_rows, LANES), f32),
            pltpu.VMEM((mine, spectra_rows, SUB, LANES), f32),
            pltpu.VMEM((mine, spectra_rows, SUB, LANES), f32),
            pltpu.VMEM(high.shape, bf16),
            pltpu.VMEM(low.shape, bf16),
            pltpu.VMEM(pick.shape[1:], bf16),
            pltpu.VMEM((QUARTERS,) + high.shape, bf16),
            pltpu.VMEM((QUARTERS,) + low.shape, bf16),
            pltpu.VMEM((2 * depth, 2 * SUB, LANES), f32),
            pltpu.VMEM((depth, stations, SUB, LANES), f32),
            pltpu.VMEM((depth, stations, SUB, LANES), f32),
            pltpu.VMEM((depth, stations, SUB, LANES), f32),
            pltpu.VMEM((depth, stations, SUB, LANES), f32),
            pltpu.VMEM((rows, SUB, LANES), f32),
            pltpu.VMEM((rows, width), bf16),
            pltpu.VMEM((rows, LAGS), f32),
            pltpu.VMEM((mine, owners, 2 * span, LAGS), bf16),
            pltpu.VMEM((mine, owners, 2 * span, LAGS), bf16),
            pltpu.VMEM((2, span, LAGS), f32),
            pltpu.VMEM((mine, wide, 2, own_rows, LAGS), f32),
            pltpu.VMEM((groups, split, mine, 2, own_rows, LAGS), f32),
            pltpu.VMEM((2, periods * own_rows, LAGS), f32),
            dma((7,)),
            dma((steps,)),
            dma((groups, steps)),
            dma((groups, steps)),
            dma((2, groups)),
            dma((2, groups)),
            dma((owners,)),
            dma((owners,)),
            dma((mine, owners)),
            dma((mine, owners)),
            dma((mine, wide)),
            dma((groups, split, mine)),
        ],
        compiler_params=pltpu.CompilerParams(collective_id=0, has_side_effects=True, vmem_limit_bytes=60 << 20),
        name="correlate",
    )(
        x, flags, poly_index.transpose(0, 2, 1), delay_model.T, partner_order,
        jnp.asarray(high), jnp.asarray(low), jnp.asarray(pick), pcos, psin,
    )
    return out.reshape(2, own_rows, periods, LAGS)


def solution(mesh):
    return jax.shard_map(
        per_device,
        mesh=mesh,
        in_specs=(
            P("stn", None, "tm", None, None),
            P("stn", None, "tm", None),
            P("stn", None, "tm"),
            P(),
            P(),
        ),
        out_specs=P(None, ("stn", "tm"), None, None),
        check_vma=False,
    )
```

time: 74.7 us -> 68.6 us (0.918)
  local copies, waits for them, and re-layouts: 4.07 us -> 1.57 us
  other arithmetic: 2.02 us -> 0 us
  Pallas kernels: 68.2 us -> 66.7 us
    pallas_call x1, Pallas kernels: 68.2 us -> 66.7 us  [per_device(): pl.pallas_call(functools.partial(kernel, (groups, owners, stations, perio...]
    reduce_sum x1 -> x0, other arithmetic: 1 us -> none  [per_device(): jnp.sum(jnp.where(onehot, delay_model[:, n], 0.0), axis=-1)]
    convert_element_type x1 -> x0, other arithmetic: 0.94 us -> none  [per_device(): w = (1.0 - flags.astype(jnp.float32)).astype(jnp.bfloat16)]
    squeeze x1 -> x0, local copies, waits for them, and re-layouts: 0.8 us -> none  [per_device(): delay_model[:, n]]
where the time goes in v2:
time: 68.6 us; the launch traced here: 68.3 us
  Pallas kernels  66.7 us (97%)
  local copies, waits for them, and re-layouts  1.57 us (2%)
    pallas_call x1, Pallas kernels, per_device(): pl.pallas_call(functools.partial(kernel, (groups, owners, stations, perio...  66.7 us
    unnamed x1, local copies, waits for them, and re-layouts  1.57 us

profile of v2, /device:TPU:0, one launch (start us, length us, event | category | flops | bytes accessed | tf_op | source)
XLA Modules:
  0.0 68.3 jit_solution(1568320596279541471)
XLA Ops:
  0.0 66.7 %correlate.1 = f32[2,64,256]{2,1,0:T(8,128)} custom-call(bf16[8,8,4,64,128]{4,3,2,1,0:T(8,128)(2,1)} %bitcast.8, s32[8,8,4,32]{3,2,1,0:T(4,128)} %flags_hbm.1, s32[8,4,8]{2,1,0:T(4,128)} %bitcast.10, f32[3,64]{1,0:T(4,128)} %bitcast.11, s32[16]{0:T(128)} %partner_ref.1, bf16[1024,256]{1,0:T(8,128)(2,1)} %constant.12.clone.high_hbm, ...), custom_call_target="tpu_custom_call" | custom-call | tf_op jit(solution)/shard_map/correlate/pallas_call | solution.py:548
  66.7 1.6 %copy.13 = f32[2,8,8,256]{3,2,1,0:T(8,128)} copy(f32[2,8,8,256]{3,2,1,0:T(8,128)} %bitcast.9) | data formatting | bytes 262144

commit v3 on v2

--- a/solution.py
+++ b/solution.py
@@ -28,46 +28,85 @@
 
 
 def pair_rows(stations):
-    tiles = stations // TILE
-    off = [(x * TILE, y * TILE) for x in range(tiles) for y in range(x + 1, tiles)]
-    real, imag = {}, {}
-    for x, y in off:
-        for i in range(TILE):
-            for j in range(TILE):
-                real[x + i, y + j] = len(real)
-    for x in range(tiles):
-        for i in range(TILE):
-            for j in range(i, TILE):
-                real[x * TILE + i, x * TILE + j] = len(real)
-    top = len(real)
-    for x, y in off:
-        for i in range(TILE):
-            for j in range(TILE):
-                imag[x + i, y + j] = top + len(imag)
-    for x in range(tiles):
-        for i in range(TILE):
-            for j in range(i + 1, TILE):
-                imag[x * TILE + i, x * TILE + j] = top + len(imag)
-    return off, real, imag
-
-
-def pick_matrix(stations, groups, owners):
-    _, real, imag = pair_rows(stations)
+    last = stations - TILE
+    kinds = []
+    real, imag, order = {}, {}, {}
+    row = 0
+    for late in (False, True):
+        off = [(x, y) for x in range(0, stations, TILE) for y in range(x + TILE, stations, TILE) if (y == last) == late]
+        same = [last] if late else list(range(0, last, TILE))
+        for part in (real, imag):
+            skip = 0 if part is real else 1
+            start = row
+            keys = [(x + i, y + j) for x, y in off for i in range(TILE) for j in range(TILE)]
+            keys += [(x + i, x + j) for x in same for i in range(TILE) for j in range(i + skip, TILE)]
+            for key in keys:
+                part[key] = row
+                row += 1
+                if part is real:
+                    order[key] = len(order)
+        kinds.append((off, same))
+    return kinds, real, imag, order
+
+
+def late_first(local):
+    return local // 4 if local >= 2 * TILE else 0
+
+
+def relative(station, plane, groups, local):
+    slot = (station // local - plane) % groups
+    place = station % local
+    return slot * local + (place if slot == 0 else (place + late_first(local)) % local)
+
+
+def pick_matrices(stations, groups, owners):
+    _, real, imag, _ = pair_rows(stations)
     split = owners // stations
     wide = groups * split
     local = stations // groups
-    span = stations // split
-    pick = np.zeros((groups, owners, 2, span, stations * stations), np.float32)
+    units = stations // split // TILE
+    rows = stations * stations
+    early = (stations - TILE) ** 2
+    pick_a = np.zeros((groups, owners, units - 1, 2, TILE, rows), np.float32)
+    pick_b = np.zeros((groups, owners, 2, TILE, rows), np.float32)
+    pick_c = np.zeros((groups, TILE * split, units - 1, 2, TILE, rows), np.float32)
     for g in range(groups):
         for t in range(owners):
-            a = (t % wide // split * local + t // wide - g * local) % stations
-            for n in range(span):
-                b = (t % split * span + n - g * local) % stations
-                key = (min(a, b), max(a, b))
-                pick[g, t, 0, n, real[key]] = 1.0
-                if a != b:
-                    pick[g, t, 1, n, imag[key]] = 1.0 if a < b else -1.0
-    return pick.reshape(groups, owners * 2 * span, stations * stations).astype(jnp.bfloat16)
+            a = relative(t % wide // split * local + t // wide, g, groups, local)
+            late = a >= stations - TILE
+            for u in range(units):
+                for n in range(TILE):
+                    b = (t % split * units + u) * TILE + n
+                    key = (min(a, b), max(a, b))
+                    if u == units - 1:
+                        target = pick_b[g, t]
+                    elif late:
+                        target = pick_c[g, (a - stations + TILE) * split + t % split, u]
+                    else:
+                        target = pick_a[g, t, u]
+                    target[0, n, real[key]] = 1.0
+                    if a != b:
+                        target[1, n, imag[key]] = 1.0 if a < b else -1.0
+    pick_a = pick_a.reshape(groups, -1, rows)
+    assert not pick_a[:, :, early:].any()
+    pick_b = np.concatenate([pick_b.reshape(groups, -1, rows), pick_c.reshape(groups, -1, rows)], axis=1)
+    return pick_a[:, :, :early].astype(jnp.bfloat16), pick_b.astype(jnp.bfloat16)
+
+
+def arrivals(stations, groups):
+    local = stations // groups
+    runs = []
+    for shift in range(1, groups):
+        slot = groups - shift
+        turn = late_first(local)
+        places = [((i - turn) % local, slot * local + i) for i in range(local)]
+        for source, here in places:
+            late = here >= stations - TILE
+            if runs and runs[-1][:2] == (late, shift) and source == runs[-1][2] + runs[-1][3]:
+                runs[-1] = (late, shift, runs[-1][2], runs[-1][3] + 1, runs[-1][4])
+            else:
+                runs.append((late, shift, source, 1, here))
+    return runs
 
 
 def period_tables(periods, rows):
@@ -105,11 +144,11 @@
 
 def kernel(
     sizes,
-    x_hbm, flags_hbm, index_hbm, model_ref, partner_ref, high_hbm, low_hbm, pick_hbm, pcos_hbm, psin_hbm,
+    x_hbm, flags_hbm, index_hbm, model_ref, partner_ref, high_hbm, low_hbm, pick_a_hbm, pick_b_hbm, pcos_hbm, psin_hbm,
     out_ref,
-    xall, flags, index_ref, pcos_ref, psin_ref, wsend, dsend, wbuf, dbuf, wall, wf, wrow, acc, scale_ref, turned,
-    wide_w, dsplat, step_c, step_s, base_c, base_s, th, tl, pick, wh, wl, tmp, yr, yi, ys, yd, v_ref, vh, z_ref,
-    zs, rb, red, fs, fr, gf,
+    xall, flags, index_ref, pcos_ref, psin_ref, wsend, dsend, wbuf, dbuf, wall, wf, wrow, acc, counts, scale_ref, turned,
+    wide_w, dsplat, step_c, step_s, base_c, base_s, th, tl, pick_a, pick_b, wh, wl, tmp, yr, yi, ys, yd, v_ref, vh, z_ref,
+    zs_a, zs_b, zs_c, rb, red, fs, fr, gf,
     table_sem, own_sem, xs_sem, xr_sem, ws_sem, wr_sem, gs_sem, gr_sem, rs_sem, rr_sem, fs_sem, fr_sem,
 ):
     groups, owners, stations, periods, depth, blocks = sizes
@@ -128,6 +167,26 @@
     place = t % wide
     plane = place // split
     part = t % split
+    units = span // TILE
+    early = (stations - TILE) ** 2
+    turn_by = late_first(local)
+    runs = arrivals(stations, groups)
+    kinds, real_row, imag_row, pair_order = pair_rows(stations)
+    pairs = len(real_row)
+
+    def relative_here(station):
+        slot = (station // local - me + groups) % groups
+        return slot * local + (station % local + (slot + groups - 1) // groups * turn_by) % local
+
+    mine_a = relative_here(plane * local + home)
+    total_steps = 2 * steps
+    full = 2 * (mine - 1) * QUARTERS
+
+    def sub_step(n):
+        last = n // full if full else 1
+        i = (1 - last) * (n // 2) + last * ((mine - 1) * QUARTERS + (n + QUARTERS * 2 - full % (QUARTERS * 2)) % QUARTERS)
+        kind = (1 - last) * (n % 2) + last * ((n + total_steps - full) // QUARTERS - total_steps // QUARTERS)
+        return i, kind
 
     def band(i):
         return pl.ds(pl.multiple_of((i % QUARTERS) * 2 * SUB, 2 * SUB), 2 * SUB)
@@ -142,8 +201,8 @@
     tables = [
         pltpu.make_async_copy(source, target, table_sem.at[n])
         for n, (source, target) in enumerate((
-            (flags_hbm, flags), (index_hbm, index_ref), (high_hbm, th), (low_hbm, tl), (pick_hbm.at[me], pick),
-            (pcos_hbm, pcos_ref), (psin_hbm, psin_ref),
+            (flags_hbm, flags), (index_hbm, index_ref), (high_hbm, th), (low_hbm, tl),
+            (pick_a_hbm.at[me], pick_a), (pick_b_hbm.at[me], pick_b), (pcos_hbm, pcos_ref), (psin_hbm, psin_ref),
         ))
     ]
     barrier = pltpu.get_barrier_semaphore()
@@ -202,12 +261,13 @@
             for n, (ref, buf) in enumerate(((wsend, wbuf), (dsend, dbuf)))
         ]
 
-    def spectra_copy(shift, i):
+    def spectra_copy(n, i):
+        _, shift, source, count, here = runs[n]
         target = lax.rem(me + shift, groups)
         return pltpu.make_async_remote_copy(
-            src_ref=x_hbm.at[:, target * mine + i // QUARTERS, :, band(i), :],
-            dst_ref=xall.at[pl.ds((groups - shift) * local, local), i // QUARTERS, :, band(i), :],
-            send_sem=xs_sem.at[shift, i], recv_sem=xr_sem.at[shift, i],
+            src_ref=x_hbm.at[pl.ds(source, count), target * mine + i // QUARTERS, :, band(i), :],
+            dst_ref=xall.at[pl.ds(here, count), i // QUARTERS, :, band(i), :],
+            send_sem=xs_sem.at[n, i], recv_sem=xr_sem.at[n, i],
             device_id={"stn": target}, device_id_type=MESH,
         )
 
@@ -215,12 +275,19 @@
         for copy in small_copies(shift):
             copy.start()
 
-    def start_spectra(i, _):
-        for shift in range(1, groups):
-            spectra_copy(shift, i).start()
+    def start_spectra(n, _):
+        i, kind = sub_step(n)
+        for late in (False, True):
+
+            @pl.when(kind == int(late))
+            def _():
+                for r in range(len(runs)):
+                    if runs[r][0] == late:
+                        spectra_copy(r, i).start()
+
         return 0
 
-    lax.fori_loop(0, steps, start_spectra, 0)
+    lax.fori_loop(0, total_steps, start_spectra, 0)
 
     for copy in tables[2:]:
         copy.wait()
@@ -257,7 +324,7 @@
 
     for g in range(groups):
         for l in range(local):
-            r = (g * local + l) * depth
+            r = (g * local + (l + turn_by * min(g, 1)) % local) * depth
             wrow[r : r + depth, :] = wbuf[g, l].astype(jnp.float32)
             d = dbuf[g, l]
             for p in range(mine):
@@ -283,8 +350,6 @@
     for r in range(spectra):
         wide_w[r] = jnp.broadcast_to(w_t[:, r : r + 1], (w_t.shape[0], LANES))
 
-    off, real_row, imag_row = pair_rows(stations)
-    pairs = len(real_row)
     acc_flat = acc.reshape(pairs * SUB, LANES)
     v_flat = v_ref.reshape(rows * SUB, LANES)
 
@@ -292,31 +357,58 @@
         for shift in range(1, owners):
             gather_copy(shift, lax.rem(t + owners - shift, owners)).wait_recv()
         for n in range(owners):
-            wf[:, n * depth : (n + 1) * depth, :] = wall[n].astype(jnp.float32).reshape(stations, depth, LANES)
+            for g in range(groups):
+                turn = turn_by * min(g, 1)
+                value = wall[n, g].astype(jnp.float32)
+                at = slice(n * depth, (n + 1) * depth)
+                wf[g * local + turn : (g + 1) * local, at, :] = value[: local - turn]
+                if turn:
+                    wf[g * local : g * local + turn, at, :] = value[local - turn :]
         for a in range(stations):
             for b0 in range(a // TILE * TILE, stations, TILE):
                 b = max(a, b0)
                 count = b0 + TILE - b
                 product = wf[a][None] * wf[b : b + count]
-                m = real_row[a, b]
+                m = pair_order[a, b]
                 acc[m : m + count] = jnp.sum(product.reshape(count, owners * depth // SUB, SUB, LANES), axis=1)
         count = acc_flat[pl.ds(0, pairs, stride=SUB), :]
         for b in range(1, SUB):
             count = count + acc_flat[pl.ds(b, pairs, stride=SUB), :]
-        scale_ref[:pairs, :] = 1.0 / jnp.sqrt(jnp.maximum(count, 1.0))
-        n = len(off) * TILE * TILE
-        if n:
-            scale_ref[pairs : pairs + n, :] = scale_ref[:n, :]
-        for x in range(0, stations, TILE):
-            for i in range(TILE - 1):
-                m, q, n = real_row[x + i, x + i + 1], imag_row[x + i, x + i + 1], TILE - 1 - i
-                scale_ref[q : q + n, :] = scale_ref[m : m + n, :]
-
-    def scatter_copy(p, shift, target, source):
+        counts[...] = 1.0 / jnp.sqrt(jnp.maximum(count, 1.0))
+        for off, same in kinds:
+            pieces = []
+            if off:
+                x, y = off[0]
+                n = len(off) * TILE * TILE
+                pieces += [(real_row[x, y], pair_order[x, y], n), (imag_row[x, y], pair_order[x, y], n)]
+            for x in same:
+                if x == same[0]:
+                    n = len(same) * TILE * (TILE + 1) // 2
+                    pieces.append((real_row[x, x], pair_order[x, x], n))
+                for i in range(TILE - 1):
+                    pieces.append((imag_row[x + i, x + i + 1], pair_order[x + i, x + i + 1], TILE - 1 - i))
+            for row, source, n in pieces:
+                scale_ref[row : row + n, :] = counts[source : source + n, :]
+
+    def station_of(target):
+        return relative_here(target % wide // split * local + target // wide)
+
+    def scatter_copy(p, shift, what, target, source):
+        if what == "last":
+            src, dst = zs_b.at[p, target], rb.at[p, source, units - 1]
+        elif what == "early":
+            src, dst = zs_a.at[p, target], rb.at[p, source, pl.ds(0, units - 1)]
+        else:
+            late = (station_of(target) + TILE) % stations * split + target % split
+            src, dst = zs_c.at[p, late], rb.at[p, source, pl.ds(0, units - 1)]
+        n = int(what == "last")
         return pltpu.make_async_remote_copy(
-            src_ref=zs.at[p, target], dst_ref=rb.at[p, source], send_sem=rs_sem.at[p, shift],
-            recv_sem=rr_sem.at[p, source], device_id={"tm": lax.rem(t + shift, owners)}, device_id_type=MESH,
+            src_ref=src, dst_ref=dst, send_sem=rs_sem.at[n, p, shift],
+            recv_sem=rr_sem.at[n, p, source], device_id={"tm": lax.rem(t + shift, owners)}, device_id_type=MESH,
         )
+
+    def is_late(target):
+        return station_of(target) >= stations - TILE
 
     def final_copy(p, w, source, piece):
         return pltpu.make_async_remote_copy(
@@ -325,21 +417,28 @@
         )
 
     def reduce_period(p):
-        total = zs[p, t].astype(jnp.float32)
         for shift in range(1, owners):
             source = lax.rem(t + owners - shift, owners)
-            scatter_copy(p, shift, t, source).wait_recv()
+            scatter_copy(p, shift, "early", t, source).wait_recv()
+            scatter_copy(p, shift, "last", t, source).wait_recv()
+        late = jnp.where(is_late(t), 1.0, 0.0)
+        first = zs_a[p, t].astype(jnp.float32)
+        first += late * zs_c[p, (mine_a % TILE) * split + part].astype(jnp.float32)
+        last = zs_b[p, t].astype(jnp.float32)
         for shift in range(1, owners):
-            total = total + rb[p, lax.rem(t + owners - shift, owners)].astype(jnp.float32)
-        red[...] = total.reshape(red.shape)
+            source = lax.rem(t + owners - shift, owners)
+            first += rb[p, source, : units - 1].astype(jnp.float32)
+            last += rb[p, source, units - 1].astype(jnp.float32)
+        red[: units - 1] = first
+        red[units - 1] = last
         for w in range(wide):
             for n in range(own_rows):
-                b = partner_ref[w * own_rows + n]
+                b = relative_here(partner_ref[w * own_rows + n])
                 if split > 1:
                     keep = jnp.where(b // span == part, 1.0, 0.0)
                     b = b % span
                 for ri in range(2):
-                    row = red[ri, pl.ds(b, 1), :]
+                    row = red[b // TILE, pl.ds(ri * TILE + b % TILE, 1), :]
                     fs[p, w, ri, n : n + 1, :] = row * keep if split > 1 else row
         for w in range(wide):
             to_self = (plane == me) & (w == place)
@@ -352,18 +451,25 @@
             def _():
                 final_copy(p, w, me, part).start()
 
-    def step(i, _):
+    half = TILE // 2
+
+    def work(i, late):
         p = i // QUARTERS
         quarter = i % QUARTERS
         at = pl.ds(pl.multiple_of(p * blocks + quarter * SUB, SUB), SUB)
-
-        own_copy(i).wait()
-        for shift in range(1, groups):
-            spectra_copy(shift, i).wait_recv()
+        first_station = stations - TILE if late else 0
+        off, same = kinds[late]
+        top, size = (early, rows - early) if late else (0, early)
+
+        if not late:
+            own_copy(i).wait()
+        for n in range(len(runs)):
+            if runs[n][0] == late:
+                spectra_copy(n, i).wait_recv()
 
         def rotate(n, _):
             for j in range(2):
-                s = n * 2 + j
+                s = first_station + n * 2 + j
                 for k in range(depth):
                     r = s * depth + k
                     tmp[j * depth + k] = xall[s, p, k, band(i), :].astype(jnp.float32)
@@ -374,24 +480,23 @@
                     w = wide_w[r, at, :]
                     new_real = (w * (real * c + imag * sn)).astype(jnp.bfloat16).astype(jnp.float32)
                     new_imag = (w * (imag * c - real * sn)).astype(jnp.bfloat16).astype(jnp.float32)
-                    yr[k, s] = new_real
-                    yi[k, s] = new_imag
-                    ys[k, s] = new_real + new_imag
-                    yd[k, s] = new_real - new_imag
+                    yr[quarter, k, s] = new_real
+                    yi[quarter, k, s] = new_imag
+                    ys[quarter, k, s] = new_real + new_imag
+                    yd[quarter, k, s] = new_real - new_imag
                     pc = step_c[p, pl.ds(r, 1), :]
                     ps = step_s[p, pl.ds(r, 1), :]
                     base_c[p, r] = c * pc - sn * ps
                     base_s[p, r] = sn * pc + c * ps
             return 0
 
-        lax.fori_loop(0, stations // 2, rotate, 0)
-
-        half = TILE // 2
+        lax.fori_loop(0, (TILE if late else stations - TILE) // 2, rotate, 0)
+
         for x, y0 in off:
             for y in (y0, y0 + half):
                 for k in range(depth):
-                    ar, ai, asum = (ref[k, x : x + TILE][:, None] for ref in (yr, yi, ys))
-                    br, bi, bdiff = (ref[k, y : y + half][None] for ref in (yr, yi, yd))
+                    ar, ai, asum = (ref[quarter, k, x : x + TILE][:, None] for ref in (yr, yi, ys))
+                    br, bi, bdiff = (ref[quarter, k, y : y + half][None] for ref in (yr, yi, yd))
                     first = ar * br if k == 0 else first + ar * br
                     second = ai * bi if k == 0 else second + ai * bi
                     third = asum * bdiff if k == 0 else third + asum * bdiff
@@ -402,16 +507,16 @@
                     q = imag_row[x + n, y]
                     v_ref[m : m + half] = real[n]
                     v_ref[q : q + half] = imag[n]
-        for x in range(0, stations, TILE):
+        for x in same:
             for a in range(x, x + TILE):
                 n = x + TILE - a
                 for k in range(depth):
-                    ar, ai = yr[k, a], yi[k, a]
+                    ar, ai = yr[quarter, k, a], yi[quarter, k, a]
                     term = ar * ar + ai * ai
                     auto = term if k == 0 else auto + term
                     if n > 1:
-                        br, bi, bdiff = yr[k, a + 1 : a + n], yi[k, a + 1 : a + n], yd[k, a + 1 : a + n]
-                        asum = ys[k, a]
+                        br, bi, bdiff = (ref[quarter, k, a + 1 : a + n] for ref in (yr, yi, yd))
+                        asum = ys[quarter, k, a]
                         first = ar * br if k == 0 else first + ar * br
                         second = ai * bi if k == 0 else second + ai * bi
                         third = asum * bdiff if k == 0 else third + asum * bdiff
@@ -422,35 +527,60 @@
                     v_ref[m + 1 : m + n] = first + second
                     v_ref[q : q + n - 1] = third - (first - second)
 
-        pl.when(i == 0)(make_scale)
-        turned[...] = pltpu.roll(scale_ref[...], LANES - (p * blocks + quarter * SUB), 1)
+        if not late:
+            pl.when(i == 0)(make_scale)
+        here = slice(top, top + size)
+        turned[here] = pltpu.roll(scale_ref[here], LANES - (p * blocks + quarter * SUB), 1)
         for b in range(SUB):
-            v = v_flat[pl.ds(b, rows, stride=SUB), :] * turned[:, b : b + 1]
-            vh[:, b * LANES : (b + 1) * LANES] = v.astype(jnp.bfloat16)
-        values = dot(vh[...], wh[quarter]) + dot(vh[...], wl[quarter])
+            v = v_flat[pl.ds(top * SUB + b, size, stride=SUB), :] * turned[here, b : b + 1]
+            vh[here, b * LANES : (b + 1) * LANES] = v.astype(jnp.bfloat16)
+        values = dot(vh[here], wh[quarter]) + dot(vh[here], wl[quarter])
 
         @pl.when(quarter == 0)
         def _():
-            z_ref[...] = values
+            z_ref[here] = values
 
         @pl.when(quarter > 0)
         def _():
-            z_ref[...] += values
+            z_ref[here] += values
 
         @pl.when(quarter == QUARTERS - 1)
         def _():
-            picked = dot(pick[...], z_ref[...].astype(jnp.bfloat16)).astype(jnp.bfloat16)
-            zs[p] = picked.reshape(zs.shape[1:])
+            if late:
+                picked = dot(pick_b[...], z_ref[...].astype(jnp.bfloat16)).reshape(-1, 2 * TILE, LAGS)
+                zs_b[p] = picked[:owners].astype(jnp.bfloat16)
+                zs_c[p] = picked[owners:].reshape(zs_c.shape[1:]).astype(jnp.bfloat16)
+            else:
+                picked = dot(pick_a[...], z_ref[here].astype(jnp.bfloat16))
+                zs_a[p] = picked.reshape(zs_a.shape[1:]).astype(jnp.bfloat16)
             for shift in range(1, owners):
-                scatter_copy(p, shift, lax.rem(t + shift, owners), t).start()
-
-        @pl.when((quarter == QUARTERS - 1) & (p > 0))
+                target = lax.rem(t + shift, owners)
+                if late:
+                    scatter_copy(p, shift, "last", target, t).start()
+
+                @pl.when(is_late(target) == late)
+                def _():
+                    scatter_copy(p, shift, "late" if late else "early", target, t).start()
+
+        if late:
+            @pl.when((quarter == QUARTERS - 1) & (p > 0))
+            def _():
+                reduce_period(p - 1)
+
+    def step(n, _):
+        i, kind = sub_step(n)
+
+        @pl.when(kind == 0)
         def _():
-            reduce_period(p - 1)
+            work(i, False)
+
+        @pl.when(kind == 1)
+        def _():
+            work(i, True)
 
         return 0
 
-    lax.fori_loop(0, steps, step, 0)
+    lax.fori_loop(0, total_steps, step, 0)
     reduce_period(mine - 1)
 
     for p in range(mine):
@@ -499,15 +629,16 @@
         gather_copy(shift, t).wait_send()
 
     def sent(i, _):
-        for shift in range(1, groups):
-            spectra_copy(shift, i).wait_send()
+        for n in range(len(runs)):
+            spectra_copy(n, i).wait_send()
         return 0
 
     lax.fori_loop(0, steps, sent, 0)
 
     def scattered(p, _):
         for shift in range(1, owners):
-            scatter_copy(p, shift, lax.rem(t + shift, owners), t).wait_send()
+            scatter_copy(p, shift, "last", lax.rem(t + shift, owners), t).wait_send()
+            scatter_copy(p, shift, "early", lax.rem(t + shift, owners), t).wait_send()
         for w in range(wide):
             @pl.when(jnp.logical_not((plane == me) & (w == place)))
             def _():
@@ -538,7 +669,9 @@
     x = spectra.reshape(local, periods, depth, 2, blocks, LANES).transpose(0, 1, 2, 4, 3, 5)
     x = x.reshape(local, periods, depth, 2 * blocks, LANES)
     high, low = lag_tables(channels)
-    pick = pick_matrix(stations, groups, owners)
+    pick_a, pick_b = pick_matrices(stations, groups, owners)
+    units = span // TILE
+    runs = arrivals(stations, groups)
     pcos, psin = period_tables(periods, own_rows)
     any_spec = pl.BlockSpec(memory_space=pl.ANY)
     smem = pl.BlockSpec(memory_space=pltpu.SMEM)
@@ -548,7 +681,7 @@
     out = pl.pallas_call(
         functools.partial(kernel, (groups, owners, stations, periods, depth, blocks)),
         out_shape=jax.ShapeDtypeStruct((2, own_rows * periods, LAGS), f32),
-        in_specs=[any_spec, any_spec, any_spec, smem, smem] + [any_spec] * 5,
+        in_specs=[any_spec, any_spec, any_spec, smem, smem] + [any_spec] * 6,
         out_specs=pl.BlockSpec(memory_space=pltpu.VMEM),
         scratch_shapes=[
             pltpu.VMEM((stations, mine, depth, 2 * blocks, LANES), bf16),
@@ -564,6 +697,7 @@
             pltpu.VMEM((stations, owners * depth, lanes), f32),
             pltpu.VMEM((spectra_rows, lanes), f32),
             pltpu.VMEM((pairs, SUB, lanes), f32),
+            pltpu.VMEM((pairs, lanes), f32),
             pltpu.VMEM((rows, lanes), f32),
             pltpu.VMEM((rows, lanes), f32),
             pltpu.VMEM((spectra_rows, lanes, LANES), f32),
@@ -574,33 +708,36 @@
             pltpu.VMEM((mine, spectra_rows, SUB, LANES), f32),
             pltpu.VMEM(high.shape, bf16),
             pltpu.VMEM(low.shape, bf16),
-            pltpu.VMEM(pick.shape[1:], bf16),
+            pltpu.VMEM(pick_a.shape[1:], bf16),
+            pltpu.VMEM(pick_b.shape[1:], bf16),
             pltpu.VMEM((QUARTERS,) + high.shape, bf16),
             pltpu.VMEM((QUARTERS,) + low.shape, bf16),
             pltpu.VMEM((2 * depth, 2 * SUB, LANES), f32),
-            pltpu.VMEM((depth, stations, SUB, LANES), f32),
-            pltpu.VMEM((depth, stations, SUB, LANES), f32),
-            pltpu.VMEM((depth, stations, SUB, LANES), f32),
-            pltpu.VMEM((depth, stations, SUB, LANES), f32),
+            pltpu.VMEM((QUARTERS, depth, stations, SUB, LANES), f32),
+            pltpu.VMEM((QUARTERS, depth, stations, SUB, LANES), f32),
+            pltpu.VMEM((QUARTERS, depth, stations, SUB, LANES), f32),
+            pltpu.VMEM((QUARTERS, depth, stations, SUB, LANES), f32),
             pltpu.VMEM((rows, SUB, LANES), f32),
             pltpu.VMEM((rows, width), bf16),
             pltpu.VMEM((rows, LAGS), f32),
-            pltpu.VMEM((mine, owners, 2 * span, LAGS), bf16),
-            pltpu.VMEM((mine, owners, 2 * span, LAGS), bf16),
-            pltpu.VMEM((2, span, LAGS), f32),
+            pltpu.VMEM((mine, owners, units - 1, 2 * TILE, LAGS), bf16),
+            pltpu.VMEM((mine, owners, 2 * TILE, LAGS), bf16),
+            pltpu.VMEM((mine, TILE * split, units - 1, 2 * TILE, LAGS), bf16),
+            pltpu.VMEM((mine, owners, units, 2 * TILE, LAGS), bf16),
+            pltpu.VMEM((units, 2 * TILE, LAGS), f32),
             pltpu.VMEM((mine, wide, 2, own_rows, LAGS), f32),
             pltpu.VMEM((groups, split, mine, 2, own_rows, LAGS), f32),
             pltpu.VMEM((2, periods * own_rows, LAGS), f32),
-            dma((7,)),
+            dma((8,)),
             dma((steps,)),
-            dma((groups, steps)),
-            dma((groups, steps)),
+            dma((len(runs), steps)),
+            dma((len(runs), steps)),
             dma((2, groups)),
             dma((2, groups)),
             dma((owners,)),
             dma((owners,)),
-            dma((mine, owners)),
-            dma((mine, owners)),
+            dma((2, mine, owners)),
+            dma((2, mine, owners)),
             dma((mine, wide)),
             dma((groups, split, mine)),
         ],
@@ -608,7 +745,7 @@
         name="correlate",
     )(
         x, flags, poly_index.transpose(0, 2, 1), delay_model.T, partner_order,
-        jnp.asarray(high), jnp.asarray(low), jnp.asarray(pick), pcos, psin,
+        jnp.asarray(high), jnp.asarray(low), jnp.asarray(pick_a), jnp.asarray(pick_b), pcos, psin,
     )
     return out.reshape(2, own_rows, periods, LAGS)
 

time: 68.6 us -> 69.2 us (level)
  Pallas kernels: 66.7 us -> 67.5 us
    pallas_call x1, Pallas kernels: 66.7 us -> 67.5 us  [per_device(): pl.pallas_call(functools.partial(kernel, (groups, owners, stations, perio...]
where the time goes in v3:
time: 69.2 us; the launch traced here: 69 us
  Pallas kernels  67.5 us (98%)
  local copies, waits for them, and re-layouts  1.57 us (2%)
    pallas_call x1, Pallas kernels, per_device(): pl.pallas_call(functools.partial(kernel, (groups, owners, stations, perio...  67.5 us
    unnamed x1, local copies, waits for them, and re-layouts  1.57 us

profile of v3, /device:TPU:0, one launch (start us, length us, event | category | flops | bytes accessed | tf_op | source)
XLA Modules:
  0.0 69.0 jit_solution(15885121280154145578)
XLA Ops:
  0.0 67.5 %correlate.1 = f32[2,64,256]{2,1,0:T(8,128)} custom-call(bf16[8,8,4,64,128]{4,3,2,1,0:T(8,128)(2,1)} %bitcast.8, s32[8,8,4,32]{3,2,1,0:T(4,128)} %flags_hbm.1, s32[8,4,8]{2,1,0:T(4,128)} %bitcast.10, f32[3,64]{1,0:T(4,128)} %bitcast.11, s32[16]{0:T(128)} %partner_ref.1, bf16[1024,256]{1,0:T(8,128)(2,1)} %constant.14.clone.high_hbm, ...), custom_call_target="tpu_custom_call" | custom-call | tf_op jit(solution)/shard_map/correlate/pallas_call | solution.py:681
  67.5 1.6 %copy.14 = f32[2,8,8,256]{3,2,1,0:T(8,128)} copy(f32[2,8,8,256]{3,2,1,0:T(8,128)} %bitcast.9) | data formatting | bytes 262144

commit v4 on v3

--- a/solution.py
+++ b/solution.py
@@ -149,7 +149,7 @@
     xall, flags, index_ref, pcos_ref, psin_ref, wsend, dsend, wbuf, dbuf, wall, wf, wrow, acc, counts, scale_ref, turned,
     wide_w, dsplat, step_c, step_s, base_c, base_s, th, tl, pick_a, pick_b, wh, wl, tmp, yr, yi, ys, yd, v_ref, vh, z_ref,
     zs_a, zs_b, zs_c, rb, red, fs, fr, gf,
-    table_sem, own_sem, xs_sem, xr_sem, ws_sem, wr_sem, gs_sem, gr_sem, rs_sem, rr_sem, fs_sem, fr_sem,
+    table_sem, own_sem, xs_sem, xr_sem, ws_sem, wr_sem, gs_sem, gr_sem, rs_sem, rr_sem, fs_sem, fr_sem, up_sem, down_sem,
 ):
     groups, owners, stations, periods, depth, blocks = sizes
     local = stations // groups
@@ -191,12 +191,10 @@
     def band(i):
         return pl.ds(pl.multiple_of((i % QUARTERS) * 2 * SUB, 2 * SUB), 2 * SUB)
 
-    def own_copy(i):
-        return pltpu.make_async_copy(
-            x_hbm.at[:, me * mine + i // QUARTERS, :, band(i), :],
-            xall.at[pl.ds(0, local), i // QUARTERS, :, band(i), :],
-            own_sem.at[i],
-        )
+    own_copy = pltpu.make_async_copy(x_hbm.at[:, pl.ds(me * mine, mine)], xall.at[pl.ds(0, local)], own_sem)
+
+    def all_of(ref, sem):
+        return pltpu.make_async_copy(ref, ref, sem)
 
     tables = [
         pltpu.make_async_copy(source, target, table_sem.at[n])
@@ -206,20 +204,78 @@
         ))
     ]
     barrier = pltpu.get_barrier_semaphore()
+    is_root = (me == 0) & (t == 0)
+    others = groups * owners - 1
+
+    def tell(sem, peer):
+        pl.semaphore_signal(sem, inc=1, device_id=peer, device_id_type=MESH)
+
+    def tell_all(sem):
+        def one(n, _):
+            tell(sem, {"stn": (n + 1) // owners, "tm": (n + 1) % owners})
+            return 0
+
+        lax.fori_loop(0, others, one, 0)
+
     for shift in range(1, groups):
-        for w in range(wide):
-            peer = {"stn": lax.rem(me + shift, groups), "tm": home * wide + lax.rem(place + w, wide)}
-            pl.semaphore_signal(barrier, inc=1, device_id=peer, device_id_type=MESH)
-    for shift in range(1, owners):
-        pl.semaphore_signal(barrier, inc=1, device_id={"tm": lax.rem(t + shift, owners)}, device_id_type=MESH)
+        tell(barrier, {"stn": lax.rem(me + shift, groups)})
+
+    @pl.when(is_root)
+    def _():
+        tell_all(barrier)
+
     for copy in tables:
         copy.start()
 
-    def start_own(i, _):
-        own_copy(i).start()
+    own_copy.start()
+
+    @pl.when(is_root)
+    def _():
+        pl.semaphore_wait(barrier, groups - 1)
+
+    @pl.when(jnp.logical_not(is_root))
+    def _():
+        pl.semaphore_wait(barrier, groups)
+        tell(up_sem, {"stn": 0, "tm": 0})
+
+
+    def small_copies(shift):
+        target = lax.rem(me + shift, groups)
+        return [
+            pltpu.make_async_remote_copy(
+                src_ref=ref.at[target], dst_ref=buf.at[groups - shift], send_sem=ws_sem.at[n, shift - 1],
+                recv_sem=wr_sem.at[n, shift - 1], device_id={"stn": target}, device_id_type=MESH,
+            )
+            for n, (ref, buf) in enumerate(((wsend, wbuf), (dsend, dbuf)))
+        ]
+
+    def arrival(i, late):
+        last = i // ((mine - 1) * QUARTERS) if mine > 1 else 1
+        return i + last * QUARTERS * int(late)
+
+    def spectra_copy(n, i):
+        late, shift, source, count, here = runs[n]
+        target = lax.rem(me + shift, groups)
+        return pltpu.make_async_remote_copy(
+            src_ref=x_hbm.at[pl.ds(source, count), target * mine + i // QUARTERS, :, band(i), :],
+            dst_ref=xall.at[pl.ds(here, count), i // QUARTERS, :, band(i), :],
+            send_sem=xs_sem, recv_sem=xr_sem.at[arrival(i, late)],
+            device_id={"stn": target}, device_id_type=MESH,
+        )
+
+    def start_spectra(n, _):
+        i, kind = sub_step(n)
+        for late in (False, True):
+
+            @pl.when(kind == int(late))
+            def _():
+                for r in range(len(runs)):
+                    if runs[r][0] == late:
+                        spectra_copy(r, i).start()
+
         return 0
 
-    lax.fori_loop(0, steps, start_own, 0)
+    lax.fori_loop(0, 2, start_spectra, 0)
 
     tables[1].wait()
     index = index_ref[...]
@@ -249,45 +305,10 @@
         wsend[g] = (1.0 - both).astype(jnp.bfloat16)
     wbuf[0] = wsend[me]
     dbuf[0] = dsend[me]
-    pl.semaphore_wait(barrier, (groups - 1) * wide + owners - 1)
-
-    def small_copies(shift):
-        target = lax.rem(me + shift, groups)
-        return [
-            pltpu.make_async_remote_copy(
-                src_ref=ref.at[target], dst_ref=buf.at[groups - shift], send_sem=ws_sem.at[n, shift],
-                recv_sem=wr_sem.at[n, shift], device_id={"stn": target}, device_id_type=MESH,
-            )
-            for n, (ref, buf) in enumerate(((wsend, wbuf), (dsend, dbuf)))
-        ]
-
-    def spectra_copy(n, i):
-        _, shift, source, count, here = runs[n]
-        target = lax.rem(me + shift, groups)
-        return pltpu.make_async_remote_copy(
-            src_ref=x_hbm.at[pl.ds(source, count), target * mine + i // QUARTERS, :, band(i), :],
-            dst_ref=xall.at[pl.ds(here, count), i // QUARTERS, :, band(i), :],
-            send_sem=xs_sem.at[n, i], recv_sem=xr_sem.at[n, i],
-            device_id={"stn": target}, device_id_type=MESH,
-        )
-
     for shift in range(1, groups):
         for copy in small_copies(shift):
             copy.start()
-
-    def start_spectra(n, _):
-        i, kind = sub_step(n)
-        for late in (False, True):
-
-            @pl.when(kind == int(late))
-            def _():
-                for r in range(len(runs)):
-                    if runs[r][0] == late:
-                        spectra_copy(r, i).start()
-
-        return 0
-
-    lax.fori_loop(0, total_steps, start_spectra, 0)
+    lax.fori_loop(2, total_steps, start_spectra, 0)
 
     for copy in tables[2:]:
         copy.wait()
@@ -312,9 +333,18 @@
         for copy in small_copies(shift):
             copy.wait_recv()
 
+    @pl.when(is_root)
+    def _():
+        pl.semaphore_wait(up_sem, others)
+        tell_all(down_sem)
+
+    @pl.when(jnp.logical_not(is_root))
+    def _():
+        pl.semaphore_wait(down_sem, 1)
+
     def gather_copy(shift, source):
         return pltpu.make_async_remote_copy(
-            src_ref=wbuf, dst_ref=wall.at[source], send_sem=gs_sem.at[shift], recv_sem=gr_sem.at[source],
+            src_ref=wbuf, dst_ref=wall.at[source], send_sem=gs_sem, recv_sem=gr_sem,
             device_id={"tm": lax.rem(t + shift, owners)}, device_id_type=MESH,
         )
 
@@ -337,15 +367,15 @@
     ).astype(jnp.float32)
     spectra = stations * depth
 
-    def start_phase(n, _):
-        p = n // spectra
-        r = n % spectra
-        c, s = cos_sin_turns(dsplat[p, pl.ds(r, 1), :] * channel)
-        base_c[p, r] = c
-        base_s[p, r] = s
-        return 0
-
-    lax.fori_loop(0, mine * spectra, start_phase, 0, unroll=8)
+    def start_phases(p):
+        def one(r, _):
+            c, s = cos_sin_turns(dsplat[p, pl.ds(r, 1), :] * channel)
+            base_c[r] = c
+            base_s[r] = s
+            return 0
+
+        lax.fori_loop(0, spectra, one, 0, unroll=8)
+
     w_t = wrow[...].T
     for r in range(spectra):
         wide_w[r] = jnp.broadcast_to(w_t[:, r : r + 1], (w_t.shape[0], LANES))
@@ -354,8 +384,7 @@
     v_flat = v_ref.reshape(rows * SUB, LANES)
 
     def make_scale():
-        for shift in range(1, owners):
-            gather_copy(shift, lax.rem(t + owners - shift, owners)).wait_recv()
+        all_of(wall.at[pl.ds(0, owners - 1)], gr_sem).wait()
         for n in range(owners):
             for g in range(groups):
                 turn = turn_by * min(g, 1)
@@ -401,10 +430,9 @@
         else:
             late = (station_of(target) + TILE) % stations * split + target % split
             src, dst = zs_c.at[p, late], rb.at[p, source, pl.ds(0, units - 1)]
-        n = int(what == "last")
         return pltpu.make_async_remote_copy(
-            src_ref=src, dst_ref=dst, send_sem=rs_sem.at[n, p, shift],
-            recv_sem=rr_sem.at[n, p, source], device_id={"tm": lax.rem(t + shift, owners)}, device_id_type=MESH,
+            src_ref=src, dst_ref=dst, send_sem=rs_sem,
+            recv_sem=rr_sem.at[p], device_id={"tm": lax.rem(t + shift, owners)}, device_id_type=MESH,
         )
 
     def is_late(target):
@@ -412,15 +440,12 @@
 
     def final_copy(p, w, source, piece):
         return pltpu.make_async_remote_copy(
-            src_ref=fs.at[p, w], dst_ref=fr.at[source, piece, p], send_sem=fs_sem.at[p, w],
-            recv_sem=fr_sem.at[source, piece, p], device_id={"stn": plane, "tm": home * wide + w}, device_id_type=MESH,
+            src_ref=fs.at[w, p], dst_ref=fr.at[source * split + piece, p], send_sem=fs_sem,
+            recv_sem=fr_sem, device_id={"stn": plane, "tm": home * wide + w}, device_id_type=MESH,
         )
 
     def reduce_period(p):
-        for shift in range(1, owners):
-            source = lax.rem(t + owners - shift, owners)
-            scatter_copy(p, shift, "early", t, source).wait_recv()
-            scatter_copy(p, shift, "last", t, source).wait_recv()
+        all_of(rb.at[p, pl.ds(0, owners - 1)], rr_sem.at[p]).wait()
         late = jnp.where(is_late(t), 1.0, 0.0)
         first = zs_a[p, t].astype(jnp.float32)
         first += late * zs_c[p, (mine_a % TILE) * split + part].astype(jnp.float32)
@@ -439,13 +464,13 @@
                     b = b % span
                 for ri in range(2):
                     row = red[b // TILE, pl.ds(ri * TILE + b % TILE, 1), :]
-                    fs[p, w, ri, n : n + 1, :] = row * keep if split > 1 else row
+                    fs[w, p, ri, n : n + 1, :] = row * keep if split > 1 else row
         for w in range(wide):
             to_self = (plane == me) & (w == place)
 
             @pl.when(to_self)
             def _():
-                fr[me, part, p] = fs[p, w]
+                fr[me * split + part, p] = fs[w, p]
 
             @pl.when(jnp.logical_not(to_self))
             def _():
@@ -461,11 +486,26 @@
         off, same = kinds[late]
         top, size = (early, rows - early) if late else (0, early)
 
-        if not late:
-            own_copy(i).wait()
-        for n in range(len(runs)):
-            if runs[n][0] == late:
-                spectra_copy(n, i).wait_recv()
+        def wait_spectra(low, high):
+            piece = xall.at[pl.ds(low, high - low), p, :, band(i), :]
+            all_of(piece, xr_sem.at[arrival(i, late)]).wait()
+
+        if late:
+            @pl.when(i >= steps - QUARTERS)
+            def _():
+                wait_spectra(stations - TILE, stations)
+        else:
+            @pl.when(i < steps - QUARTERS)
+            def _():
+                wait_spectra(local, stations)
+
+            @pl.when(i >= steps - QUARTERS)
+            def _():
+                wait_spectra(local, stations - TILE)
+
+            @pl.when(quarter == 0)
+            def _():
+                start_phases(p)
 
         def rotate(n, _):
             for j in range(2):
@@ -475,8 +515,8 @@
                     tmp[j * depth + k] = xall[s, p, k, band(i), :].astype(jnp.float32)
                     real = tmp[j * depth + k, pl.ds(0, SUB, stride=2), :]
                     imag = tmp[j * depth + k, pl.ds(1, SUB, stride=2), :]
-                    c = base_c[p, r]
-                    sn = base_s[p, r]
+                    c = base_c[r]
+                    sn = base_s[r]
                     w = wide_w[r, at, :]
                     new_real = (w * (real * c + imag * sn)).astype(jnp.bfloat16).astype(jnp.float32)
                     new_imag = (w * (imag * c - real * sn)).astype(jnp.bfloat16).astype(jnp.float32)
@@ -486,8 +526,8 @@
                     yd[quarter, k, s] = new_real - new_imag
                     pc = step_c[p, pl.ds(r, 1), :]
                     ps = step_s[p, pl.ds(r, 1), :]
-                    base_c[p, r] = c * pc - sn * ps
-                    base_s[p, r] = sn * pc + c * ps
+                    base_c[r] = c * pc - sn * ps
+                    base_s[r] = sn * pc + c * ps
             return 0
 
         lax.fori_loop(0, (TILE if late else stations - TILE) // 2, rotate, 0)
@@ -580,23 +620,31 @@
 
         return 0
 
+    own_copy.wait()
     lax.fori_loop(0, total_steps, step, 0)
+    for shift in range(1, groups):
+        for copy in small_copies(shift):
+            copy.wait_send()
+    all_of(wall.at[pl.ds(0, owners - 1)], gs_sem).wait()
+    all_of(xall.at[pl.ds(local, stations - local)], xs_sem).wait()
     reduce_period(mine - 1)
-
-    for p in range(mine):
-        for g in range(groups):
-            for h in range(split):
-                from_self = (me == g) & (place == me * split + h)
-
-                @pl.when(jnp.logical_not(from_self))
-                def _():
-                    final_copy(p, 0, g, h).wait_recv()
+    all_of(rb.at[:, pl.ds(0, owners - 1)], rs_sem).wait()
+
+    @pl.when(plane == me)
+    def _():
+        all_of(fr.at[pl.ds(0, wide - 1)], fr_sem).wait()
+        all_of(fs.at[pl.ds(0, wide - 1)], fs_sem).wait()
+
+    @pl.when(plane != me)
+    def _():
+        all_of(fr, fr_sem).wait()
+        all_of(fs, fs_sem).wait()
 
     for g in range(groups):
         for p in range(mine):
-            value = fr[g, 0, p]
+            value = fr[g * split, p]
             for h in range(1, split):
-                value = value + fr[g, h, p]
+                value = value + fr[g * split + h, p]
             r = (g * mine + p) * own_rows
             gf[:, r : r + own_rows, :] = value
 
@@ -621,31 +669,6 @@
         cols = slice(side * lags, (side + 1) * lags)
         out_ref[0, :, cols] = (mix(pcos, real) + mix(psin, imag)) * factor
         out_ref[1, :, cols] = (mix(pcos, imag) - mix(psin, real)) * factor
-
-    for shift in range(1, groups):
-        for copy in small_copies(shift):
-            copy.wait_send()
-    for shift in range(1, owners):
-        gather_copy(shift, t).wait_send()
-
-    def sent(i, _):
-        for n in range(len(runs)):
-            spectra_copy(n, i).wait_send()
-        return 0
-
-    lax.fori_loop(0, steps, sent, 0)
-
-    def scattered(p, _):
-        for shift in range(1, owners):
-            scatter_copy(p, shift, "last", lax.rem(t + shift, owners), t).wait_send()
-            scatter_copy(p, shift, "early", lax.rem(t + shift, owners), t).wait_send()
-        for w in range(wide):
-            @pl.when(jnp.logical_not((plane == me) & (w == place)))
-            def _():
-                final_copy(p, w, me, part).wait_send()
-        return 0
-
-    lax.fori_loop(0, mine, scattered, 0)
 
 
 def per_device(spectra, flags, poly_index, delay_model, partner_order):
@@ -704,8 +727,8 @@
             pltpu.VMEM((mine, spectra_rows, LANES), f32),
             pltpu.VMEM((mine, spectra_rows, LANES), f32),
             pltpu.VMEM((mine, spectra_rows, LANES), f32),
-            pltpu.VMEM((mine, spectra_rows, SUB, LANES), f32),
-            pltpu.VMEM((mine, spectra_rows, SUB, LANES), f32),
+            pltpu.VMEM((spectra_rows, SUB, LANES), f32),
+            pltpu.VMEM((spectra_rows, SUB, LANES), f32),
             pltpu.VMEM(high.shape, bf16),
             pltpu.VMEM(low.shape, bf16),
             pltpu.VMEM(pick_a.shape[1:], bf16),
@@ -725,21 +748,23 @@
             pltpu.VMEM((mine, TILE * split, units - 1, 2 * TILE, LAGS), bf16),
             pltpu.VMEM((mine, owners, units, 2 * TILE, LAGS), bf16),
             pltpu.VMEM((units, 2 * TILE, LAGS), f32),
-            pltpu.VMEM((mine, wide, 2, own_rows, LAGS), f32),
-            pltpu.VMEM((groups, split, mine, 2, own_rows, LAGS), f32),
+            pltpu.VMEM((wide, mine, 2, own_rows, LAGS), f32),
+            pltpu.VMEM((wide, mine, 2, own_rows, LAGS), f32),
             pltpu.VMEM((2, periods * own_rows, LAGS), f32),
             dma((8,)),
-            dma((steps,)),
-            dma((len(runs), steps)),
-            dma((len(runs), steps)),
-            dma((2, groups)),
-            dma((2, groups)),
-            dma((owners,)),
-            dma((owners,)),
-            dma((2, mine, owners)),
-            dma((2, mine, owners)),
-            dma((mine, wide)),
-            dma((groups, split, mine)),
+            dma,
+            dma,
+            dma((steps + QUARTERS,)),
+            dma((2, groups - 1)),
+            dma((2, groups - 1)),
+            dma,
+            dma,
+            dma,
+            dma((mine,)),
+            dma,
+            dma,
+            pltpu.SemaphoreType.REGULAR,
+            pltpu.SemaphoreType.REGULAR,
         ],
         compiler_params=pltpu.CompilerParams(collective_id=0, has_side_effects=True, vmem_limit_bytes=60 << 20),
         name="correlate",

time: 69.2 us -> 65.2 us (0.942)
  Pallas kernels: 67.5 us -> 63.5 us
    pallas_call x1, Pallas kernels: 67.5 us -> 63.5 us  [per_device(): pl.pallas_call(functools.partial(kernel, (groups, owners, stations, perio...]
where the time goes in v4:
time: 65.2 us; the launch traced here: 65 us
  Pallas kernels  63.5 us (97%)
  local copies, waits for them, and re-layouts  1.57 us (2%)
    pallas_call x1, Pallas kernels, per_device(): pl.pallas_call(functools.partial(kernel, (groups, owners, stations, perio...  63.5 us
    unnamed x1, local copies, waits for them, and re-layouts  1.57 us

profile of v4, /device:TPU:0, one launch (start us, length us, event | category | flops | bytes accessed | tf_op | source)
XLA Modules:
  0.0 65.0 jit_solution(14413898360472888368)
XLA Ops:
  0.0 63.5 %correlate.1 = f32[2,64,256]{2,1,0:T(8,128)} custom-call(bf16[8,8,4,64,128]{4,3,2,1,0:T(8,128)(2,1)} %bitcast.8, s32[8,8,4,32]{3,2,1,0:T(4,128)} %flags_hbm.1, s32[8,4,8]{2,1,0:T(4,128)} %bitcast.10, f32[3,64]{1,0:T(4,128)} %bitcast.11, s32[16]{0:T(128)} %partner_ref.1, bf16[1024,256]{1,0:T(8,128)(2,1)} %constant.14.clone.high_hbm, ...), custom_call_target="tpu_custom_call" | custom-call | tf_op jit(solution)/shard_map/correlate/pallas_call | solution.py:704
  63.5 1.6 %copy.14 = f32[2,8,8,256]{3,2,1,0:T(8,128)} copy(f32[2,8,8,256]{3,2,1,0:T(8,128)} %bitcast.9) | data formatting | bytes 262144

commit v5 on v4

--- a/solution.py
+++ b/solution.py
@@ -109,18 +109,6 @@
     return runs
 
 
-def period_tables(periods, rows):
-    idx = np.arange(periods)
-    angle = (idx[:, None] * idx[None, :] % periods) * (2.0 * np.pi / periods)
-    eye = np.eye(rows)
-
-    def table(m):
-        wide = np.einsum("rp,nm->nrpm", m, eye).reshape(rows * periods, periods * rows)
-        return jnp.asarray(wide.astype(np.float32))
-
-    return table(np.cos(angle)), table(np.sin(angle))
-
-
 def dot(a, b):
     return jnp.dot(a, b, preferred_element_type=jnp.float32)
 
@@ -144,9 +132,9 @@
 
 def kernel(
     sizes,
-    x_hbm, flags_hbm, index_hbm, model_ref, partner_ref, high_hbm, low_hbm, pick_a_hbm, pick_b_hbm, pcos_hbm, psin_hbm,
+    x_hbm, flags_hbm, index_hbm, model_hbm, partner_hbm, high_hbm, low_hbm, pick_a_hbm, pick_b_hbm,
     out_ref,
-    xall, flags, index_ref, pcos_ref, psin_ref, wsend, dsend, wbuf, dbuf, wall, wf, wrow, acc, counts, scale_ref, turned,
+    xall, flags, index_ref, model_ref, partner_ref, wsend, dsend, wbuf, dbuf, wall, wf, wrow, acc, counts, scale_ref, turned,
     wide_w, dsplat, step_c, step_s, base_c, base_s, th, tl, pick_a, pick_b, wh, wl, tmp, yr, yi, ys, yd, v_ref, vh, z_ref,
     zs_a, zs_b, zs_c, rb, red, fs, fr, gf,
     table_sem, own_sem, xs_sem, xr_sem, ws_sem, wr_sem, gs_sem, gr_sem, rs_sem, rr_sem, fs_sem, fr_sem, up_sem, down_sem,
@@ -200,7 +188,8 @@
         pltpu.make_async_copy(source, target, table_sem.at[n])
         for n, (source, target) in enumerate((
             (flags_hbm, flags), (index_hbm, index_ref), (high_hbm, th), (low_hbm, tl),
-            (pick_a_hbm.at[me], pick_a), (pick_b_hbm.at[me], pick_b), (pcos_hbm, pcos_ref), (psin_hbm, psin_ref),
+            (pick_a_hbm.at[me], pick_a), (pick_b_hbm.at[me], pick_b), (partner_hbm, partner_ref),
+            (model_hbm, model_ref),
         ))
     ]
     barrier = pltpu.get_barrier_semaphore()
@@ -278,6 +267,7 @@
     lax.fori_loop(0, 2, start_spectra, 0)
 
     tables[1].wait()
+    tables[7].wait()
     index = index_ref[...]
 
     def look_up(n, coef):
@@ -310,7 +300,7 @@
             copy.start()
     lax.fori_loop(2, total_steps, start_spectra, 0)
 
-    for copy in tables[2:]:
+    for copy in tables[2:7]:
         copy.wait()
     lag = lax.broadcasted_iota(jnp.int32, (1, lags), 1) + 1
     for quarter in range(QUARTERS):
@@ -441,7 +431,7 @@
     def final_copy(p, w, source, piece):
         return pltpu.make_async_remote_copy(
             src_ref=fs.at[w, p], dst_ref=fr.at[source * split + piece, p], send_sem=fs_sem,
-            recv_sem=fr_sem, device_id={"stn": plane, "tm": home * wide + w}, device_id_type=MESH,
+            recv_sem=fr_sem.at[p // (mine - 1) if mine > 1 else 1], device_id={"stn": plane, "tm": home * wide + w}, device_id_type=MESH,
         )
 
     def reduce_period(p):
@@ -466,13 +456,13 @@
                     row = red[b // TILE, pl.ds(ri * TILE + b % TILE, 1), :]
                     fs[w, p, ri, n : n + 1, :] = row * keep if split > 1 else row
         for w in range(wide):
-            to_self = (plane == me) & (w == place)
-
-            @pl.when(to_self)
+            @pl.when((plane == me) & (w == place))
             def _():
                 fr[me * split + part, p] = fs[w, p]
 
-            @pl.when(jnp.logical_not(to_self))
+    def start_final(p):
+        for w in range(wide):
+            @pl.when(jnp.logical_not((plane == me) & (w == place)))
             def _():
                 final_copy(p, w, me, part).start()
 
@@ -622,53 +612,94 @@
 
     own_copy.wait()
     lax.fori_loop(0, total_steps, step, 0)
+    for p in range(mine - 1):
+        start_final(p)
     for shift in range(1, groups):
         for copy in small_copies(shift):
             copy.wait_send()
     all_of(wall.at[pl.ds(0, owners - 1)], gs_sem).wait()
+    reduce_period(mine - 1)
+    start_final(mine - 1)
     all_of(xall.at[pl.ds(local, stations - local)], xs_sem).wait()
-    reduce_period(mine - 1)
     all_of(rb.at[:, pl.ds(0, owners - 1)], rs_sem).wait()
+
+    flip = (
+        lax.broadcasted_iota(jnp.int32, (lags, lags), 0) + lax.broadcasted_iota(jnp.int32, (lags, lags), 1) == lags - 1
+    ).astype(jnp.bfloat16)
+    factor = 1.0 / math.sqrt(periods * blocks * LANES)
+
+    def wait_final(which, count):
+        @pl.when(plane == me)
+        def _():
+            all_of(fr.at[pl.ds(0, wide - 1), pl.ds(0, count)], fr_sem.at[which]).wait()
+
+        @pl.when(plane != me)
+        def _():
+            all_of(fr.at[:, pl.ds(0, count)], fr_sem.at[which]).wait()
+
+    def transform(first, last):
+        values, low = [], []
+        for g in range(groups):
+            for p in range(first, last):
+                value = fr[g * split, p]
+                for h in range(1, split):
+                    value = value + fr[g * split + h, p]
+                rc, rs = value[0, :, :lags], value[0, :, lags:]
+                ic, im_s = value[1, :, :lags], value[1, :, lags:]
+                values.append((g * mine + p, rc + im_s, ic - rs))
+                low += [rc - im_s, ic + rs]
+        low = jnp.concatenate(low, axis=0) if len(low) > 1 else low[0]
+        high = low.astype(jnp.bfloat16)
+        rest = low - high.astype(jnp.float32)
+        middle = rest.astype(jnp.bfloat16)
+        rest = (rest - middle.astype(jnp.float32)).astype(jnp.bfloat16)
+        low = dot(high, flip) + dot(middle, flip) + dot(rest, flip)
+        sums = []
+        for r in range(periods):
+            parts = []
+            for side in range(2):
+                real = imag = None
+                for n, (p, re, im) in enumerate(values):
+                    if side == 0:
+                        re = low[2 * n * own_rows : (2 * n + 1) * own_rows]
+                        im = low[(2 * n + 1) * own_rows : (2 * n + 2) * own_rows]
+                    c = math.cos(2.0 * math.pi * (p * r % periods) / periods) * factor
+                    s = math.sin(2.0 * math.pi * (p * r % periods) / periods) * factor
+                    if abs(c) < 1e-9 * factor:
+                        new_re, new_im = s * im, -s * re
+                    elif abs(s) < 1e-9 * factor:
+                        new_re, new_im = c * re, c * im
+                    else:
+                        new_re, new_im = c * re + s * im, c * im - s * re
+                    real = new_re if real is None else real + new_re
+                    imag = new_im if imag is None else imag + new_im
+                parts.append((real, imag))
+            sums.append(parts)
+        return sums
+
+    if mine > 1:
+        wait_final(0, mine - 1)
+        for r, parts in enumerate(transform(0, mine - 1)):
+            for side, (real, imag) in enumerate(parts):
+                cols = slice(side * lags, (side + 1) * lags)
+                gf[0, r, :, cols] = real
+                gf[1, r, :, cols] = imag
+    wait_final(1, 1)
+    for r, parts in enumerate(transform(mine - 1, mine)):
+        for side, pair in enumerate(parts):
+            cols = slice(side * lags, (side + 1) * lags)
+            for n, value in enumerate(pair):
+                if mine > 1:
+                    value = value + gf[n, r, :, cols]
+                out_ref[n, pl.ds(side * periods + r, own_rows, stride=2 * periods), :] = value
 
     @pl.when(plane == me)
     def _():
-        all_of(fr.at[pl.ds(0, wide - 1)], fr_sem).wait()
         all_of(fs.at[pl.ds(0, wide - 1)], fs_sem).wait()
 
     @pl.when(plane != me)
     def _():
-        all_of(fr, fr_sem).wait()
         all_of(fs, fs_sem).wait()
-
-    for g in range(groups):
-        for p in range(mine):
-            value = fr[g * split, p]
-            for h in range(1, split):
-                value = value + fr[g * split + h, p]
-            r = (g * mine + p) * own_rows
-            gf[:, r : r + own_rows, :] = value
-
-    highest = lax.Precision.HIGHEST
-    rc, rs = gf[0, :, :lags], gf[0, :, lags:]
-    ic, im_s = gf[1, :, :lags], gf[1, :, lags:]
-    flip = (
-        lax.broadcasted_iota(jnp.int32, (lags, lags), 0) + lax.broadcasted_iota(jnp.int32, (lags, lags), 1) == lags - 1
-    ).astype(jnp.float32)
-    pcos = pcos_ref[...]
-    psin = psin_ref[...]
-    factor = 1.0 / math.sqrt(periods * blocks * LANES)
-
-    def mix(m, v):
-        return jnp.dot(m, v, precision=highest, preferred_element_type=jnp.float32)
-
-    for side in range(2):
-        if side == 0:
-            real, imag = mix(rc - im_s, flip), mix(ic + rs, flip)
-        else:
-            real, imag = rc + im_s, ic - rs
-        cols = slice(side * lags, (side + 1) * lags)
-        out_ref[0, :, cols] = (mix(pcos, real) + mix(psin, imag)) * factor
-        out_ref[1, :, cols] = (mix(pcos, imag) - mix(psin, real)) * factor
 
 
 def per_device(spectra, flags, poly_index, delay_model, partner_order):
@@ -695,23 +726,21 @@
     pick_a, pick_b = pick_matrices(stations, groups, owners)
     units = span // TILE
     runs = arrivals(stations, groups)
-    pcos, psin = period_tables(periods, own_rows)
-    any_spec = pl.BlockSpec(memory_space=pl.ANY)
-    smem = pl.BlockSpec(memory_space=pltpu.SMEM)
+    hbm = pl.BlockSpec(memory_space=pltpu.HBM)
     f32, bf16, i32 = jnp.float32, jnp.bfloat16, jnp.int32
     spectra_rows = stations * depth
     dma = pltpu.SemaphoreType.DMA
     out = pl.pallas_call(
         functools.partial(kernel, (groups, owners, stations, periods, depth, blocks)),
-        out_shape=jax.ShapeDtypeStruct((2, own_rows * periods, LAGS), f32),
-        in_specs=[any_spec, any_spec, any_spec, smem, smem] + [any_spec] * 6,
+        out_shape=jax.ShapeDtypeStruct((2, own_rows * 2 * periods, LAGS // 2), f32),
+        in_specs=[hbm] * 9,
         out_specs=pl.BlockSpec(memory_space=pltpu.VMEM),
         scratch_shapes=[
             pltpu.VMEM((stations, mine, depth, 2 * blocks, LANES), bf16),
             pltpu.VMEM(flags.shape, i32),
             pltpu.VMEM((local, depth, periods), i32),
-            pltpu.VMEM(pcos.shape, f32),
-            pltpu.VMEM(psin.shape, f32),
+            pltpu.SMEM(delay_model.shape[::-1], f32),
+            pltpu.SMEM(partner_order.shape, i32),
             pltpu.VMEM((groups, local, depth, lanes), bf16),
             pltpu.VMEM((groups, local, depth, LANES), f32),
             pltpu.VMEM((groups, local, depth, lanes), bf16),
@@ -750,7 +779,7 @@
             pltpu.VMEM((units, 2 * TILE, LAGS), f32),
             pltpu.VMEM((wide, mine, 2, own_rows, LAGS), f32),
             pltpu.VMEM((wide, mine, 2, own_rows, LAGS), f32),
-            pltpu.VMEM((2, periods * own_rows, LAGS), f32),
+            pltpu.VMEM((2, periods, own_rows, LAGS), f32),
             dma((8,)),
             dma,
             dma,
@@ -762,16 +791,20 @@
             dma,
             dma((mine,)),
             dma,
-            dma,
+            dma((2,)),
             pltpu.SemaphoreType.REGULAR,
             pltpu.SemaphoreType.REGULAR,
         ],
-        compiler_params=pltpu.CompilerParams(collective_id=0, has_side_effects=True, vmem_limit_bytes=60 << 20),
+        compiler_params=pltpu.CompilerParams(collective_id=0, has_side_effects=True, vmem_limit_bytes=40 << 20),
         name="correlate",
-    )(
-        x, flags, poly_index.transpose(0, 2, 1), delay_model.T, partner_order,
-        jnp.asarray(high), jnp.asarray(low), jnp.asarray(pick_a), jnp.asarray(pick_b), pcos, psin,
-    )
+    )(*(
+        pltpu.with_memory_space_constraint(value, pltpu.HBM)
+        for value in (
+            x, flags, poly_index.transpose(0, 2, 1), delay_model.T, partner_order,
+            jnp.asarray(high), jnp.asarray(low), jnp.asarray(pick_a), jnp.asarray(pick_b),
+        )
+    ))
+    out = out.reshape(2, own_rows, 2, periods, LAGS // 2).transpose(0, 1, 3, 2, 4)
     return out.reshape(2, own_rows, periods, LAGS)
 
 

time: 65.2 us -> 62.6 us (0.960)
  Pallas kernels: 63.5 us -> 61.8 us
  local copies, waits for them, and re-layouts: 1.57 us -> 0.66 us
    pallas_call x1, Pallas kernels: 63.5 us -> 61.8 us  [per_device(): pl.pallas_call(functools.partial(kernel, (groups, owners, stations, perio...]
    unnamed x1, local copies, waits for them, and re-layouts: 1.57 us -> 0.66 us
where the time goes in v5:
time: 62.6 us; the launch traced here: 62.4 us
  Pallas kernels  61.8 us (99%)
  local copies, waits for them, and re-layouts  0.66 us (1%)
    pallas_call x1, Pallas kernels, per_device(): pl.pallas_call(functools.partial(kernel, (groups, owners, stations, perio...  61.8 us

profile of v5, /device:TPU:0, one launch (start us, length us, event | category | flops | bytes accessed | tf_op | source)
XLA Modules:
  0.0 62.4 jit_solution(12158866750416771580)
XLA Ops:
  0.0 61.8 %correlate.1 = f32[2,128,128]{2,1,0:T(8,128)S(1)} custom-call(bf16[8,8,4,64,128]{4,3,2,1,0:T(8,128)(2,1)} %bitcast.13, s32[8,8,4,32]{3,2,1,0:T(4,128)} %flags_hbm.1, s32[8,4,8]{2,1,0:T(4,128)} %bitcast.14, f32[3,64]{1,0:T(4,128)} %bitcast.15, s32[16]{0:T(128)} %partner_hbm.1, bf16[1024,256]{1,0:T(8,128)(2,1)} %constant.8.clone.high_hbm, ...), custom_call_target="tpu_custom_call" | custom-call | tf_op jit(solution)/shard_map/correlate/pallas_call | solution.py:733
  61.8 0.7 %copy.12 = f32[2,8,8,256]{3,2,1,0:T(8,128)} copy(f32[2,8,8,256]{3,2,1,0:T(8,128)S(1)} %bitcast.12) | data formatting | bytes 262144

commit v6 on v5

--- a/solution.py
+++ b/solution.py
@@ -72,7 +72,7 @@
     pick_c = np.zeros((groups, TILE * split, units - 1, 2, TILE, rows), np.float32)
     for g in range(groups):
         for t in range(owners):
-            a = relative(t % wide // split * local + t // wide, g, groups, local)
+            a = relative((t % wide // split + g) % groups * local + t // wide, g, groups, local)
             late = a >= stations - TILE
             for u in range(units):
                 for n in range(TILE):
@@ -153,7 +153,7 @@
     t = lax.axis_index("tm")
     home = t // wide
     place = t % wide
-    plane = place // split
+    plane = (place // split + me) % groups
     part = t % split
     units = span // TILE
     early = (stations - TILE) ** 2
@@ -300,6 +300,11 @@
             copy.start()
     lax.fori_loop(2, total_steps, start_spectra, 0)
 
+    @pl.when(is_root)
+    def _():
+        pl.semaphore_wait(up_sem, others)
+        tell_all(down_sem)
+
     for copy in tables[2:7]:
         copy.wait()
     lag = lax.broadcasted_iota(jnp.int32, (1, lags), 1) + 1
@@ -322,11 +327,6 @@
     for shift in range(1, groups):
         for copy in small_copies(shift):
             copy.wait_recv()
-
-    @pl.when(is_root)
-    def _():
-        pl.semaphore_wait(up_sem, others)
-        tell_all(down_sem)
 
     @pl.when(jnp.logical_not(is_root))
     def _():
@@ -371,7 +371,7 @@
         wide_w[r] = jnp.broadcast_to(w_t[:, r : r + 1], (w_t.shape[0], LANES))
 
     acc_flat = acc.reshape(pairs * SUB, LANES)
-    v_flat = v_ref.reshape(rows * SUB, LANES)
+    v_flat = v_ref.reshape(QUARTERS * rows * SUB, LANES)
 
     def make_scale():
         all_of(wall.at[pl.ds(0, owners - 1)], gr_sem).wait()
@@ -410,7 +410,7 @@
                 scale_ref[row : row + n, :] = counts[source : source + n, :]
 
     def station_of(target):
-        return relative_here(target % wide // split * local + target // wide)
+        return relative_here((target % wide // split + me) % groups * local + target // wide)
 
     def scatter_copy(p, shift, what, target, source):
         if what == "last":
@@ -468,13 +468,12 @@
 
     half = TILE // 2
 
-    def work(i, late):
+    def products(i, late):
         p = i // QUARTERS
         quarter = i % QUARTERS
         at = pl.ds(pl.multiple_of(p * blocks + quarter * SUB, SUB), SUB)
         first_station = stations - TILE if late else 0
         off, same = kinds[late]
-        top, size = (early, rows - early) if late else (0, early)
 
         def wait_spectra(low, high):
             piece = xall.at[pl.ds(low, high - low), p, :, band(i), :]
@@ -535,8 +534,8 @@
                 for n in range(TILE):
                     m = real_row[x + n, y]
                     q = imag_row[x + n, y]
-                    v_ref[m : m + half] = real[n]
-                    v_ref[q : q + half] = imag[n]
+                    v_ref[quarter, m : m + half] = real[n]
+                    v_ref[quarter, q : q + half] = imag[n]
         for x in same:
             for a in range(x, x + TILE):
                 n = x + TILE - a
@@ -551,18 +550,20 @@
                         second = ai * bi if k == 0 else second + ai * bi
                         third = asum * bdiff if k == 0 else third + asum * bdiff
                 m = real_row[a, a]
-                v_ref[m] = auto
+                v_ref[quarter, m] = auto
                 if n > 1:
                     q = imag_row[a, a + 1]
-                    v_ref[m + 1 : m + n] = first + second
-                    v_ref[q : q + n - 1] = third - (first - second)
-
-        if not late:
-            pl.when(i == 0)(make_scale)
+                    v_ref[quarter, m + 1 : m + n] = first + second
+                    v_ref[quarter, q : q + n - 1] = third - (first - second)
+
+    def lag_sums(i, which):
+        p = i // QUARTERS
+        quarter = i % QUARTERS
+        top, size = {"all": (0, rows), "early": (0, early), "late": (early, rows - early)}[which]
         here = slice(top, top + size)
         turned[here] = pltpu.roll(scale_ref[here], LANES - (p * blocks + quarter * SUB), 1)
         for b in range(SUB):
-            v = v_flat[pl.ds(top * SUB + b, size, stride=SUB), :] * turned[here, b : b + 1]
+            v = v_flat[pl.ds(quarter * (rows * SUB) + top * SUB + b, size, stride=SUB), :] * turned[here, b : b + 1]
             vh[here, b * LANES : (b + 1) * LANES] = v.astype(jnp.bfloat16)
         values = dot(vh[here], wh[quarter]) + dot(vh[here], wl[quarter])
 
@@ -576,42 +577,69 @@
 
         @pl.when(quarter == QUARTERS - 1)
         def _():
-            if late:
+            if which != "early":
                 picked = dot(pick_b[...], z_ref[...].astype(jnp.bfloat16)).reshape(-1, 2 * TILE, LAGS)
                 zs_b[p] = picked[:owners].astype(jnp.bfloat16)
                 zs_c[p] = picked[owners:].reshape(zs_c.shape[1:]).astype(jnp.bfloat16)
-            else:
-                picked = dot(pick_a[...], z_ref[here].astype(jnp.bfloat16))
+            if which != "late":
+                picked = dot(pick_a[...], z_ref[:early].astype(jnp.bfloat16))
                 zs_a[p] = picked.reshape(zs_a.shape[1:]).astype(jnp.bfloat16)
             for shift in range(1, owners):
                 target = lax.rem(t + shift, owners)
-                if late:
+                if which != "early":
                     scatter_copy(p, shift, "last", target, t).start()
 
-                @pl.when(is_late(target) == late)
-                def _():
-                    scatter_copy(p, shift, "late" if late else "early", target, t).start()
-
-        if late:
+                    @pl.when(is_late(target))
+                    def _():
+                        scatter_copy(p, shift, "late", target, t).start()
+
+                if which != "late":
+                    @pl.when(jnp.logical_not(is_late(target)))
+                    def _():
+                        scatter_copy(p, shift, "early", target, t).start()
+
+        if which != "early" and mine > 1:
             @pl.when((quarter == QUARTERS - 1) & (p > 0))
             def _():
                 reduce_period(p - 1)
 
-    def step(n, _):
-        i, kind = sub_step(n)
-
-        @pl.when(kind == 0)
+    normal = steps - QUARTERS
+    ahead = 3 if normal else 0
+
+    def step(m, _):
+        stages = (normal + ahead) // ahead
+        i = m - ahead * ((m // ahead + stages - 1) // stages)
+
+        @pl.when((m < ahead) | (m >= 2 * ahead))
         def _():
-            work(i, False)
-
-        @pl.when(kind == 1)
+            products(i, False)
+            products(i, True)
+
+        pl.when(m == ahead)(make_scale)
+
+        @pl.when(m >= ahead)
         def _():
-            work(i, True)
+            lag_sums(i, "all")
 
         return 0
 
+    def last_step(n, _):
+        i = normal + n % QUARTERS
+        for late in (False, True):
+
+            @pl.when(n // QUARTERS == int(late))
+            def _():
+                products(i, late)
+                lag_sums(i, "late" if late else "early")
+
+        return 0
+
     own_copy.wait()
-    lax.fori_loop(0, total_steps, step, 0)
+    if normal:
+        lax.fori_loop(0, normal + ahead, step, 0)
+    else:
+        make_scale()
+    lax.fori_loop(0, 2 * QUARTERS, last_step, 0)
     for p in range(mine - 1):
         start_final(p)
     for shift in range(1, groups):
@@ -769,7 +797,7 @@
             pltpu.VMEM((QUARTERS, depth, stations, SUB, LANES), f32),
             pltpu.VMEM((QUARTERS, depth, stations, SUB, LANES), f32),
             pltpu.VMEM((QUARTERS, depth, stations, SUB, LANES), f32),
-            pltpu.VMEM((rows, SUB, LANES), f32),
+            pltpu.VMEM((QUARTERS, rows, SUB, LANES), f32),
             pltpu.VMEM((rows, width), bf16),
             pltpu.VMEM((rows, LAGS), f32),
             pltpu.VMEM((mine, owners, units - 1, 2 * TILE, LAGS), bf16),

time: 62.6 us -> 61.1 us (0.976)
  Pallas kernels: 61.8 us -> 60.3 us
    pallas_call x1, Pallas kernels: 61.8 us -> 60.3 us  [per_device(): pl.pallas_call(functools.partial(kernel, (groups, owners, stations, perio...]
where the time goes in v6:
time: 61.1 us; the launch traced here: 60.9 us
  Pallas kernels  60.3 us (99%)
  local copies, waits for them, and re-layouts  0.66 us (1%)
    pallas_call x1, Pallas kernels, per_device(): pl.pallas_call(functools.partial(kernel, (groups, owners, stations, perio...  60.3 us

profile of v6, /device:TPU:0, one launch (start us, length us, event | category | flops | bytes accessed | tf_op | source)
XLA Modules:
  0.0 60.9 jit_solution(8380160287441642608)
XLA Ops:
  0.0 60.3 %correlate.1 = f32[2,128,128]{2,1,0:T(8,128)S(1)} custom-call(bf16[8,8,4,64,128]{4,3,2,1,0:T(8,128)(2,1)} %bitcast.13, s32[8,8,4,32]{3,2,1,0:T(4,128)} %flags_hbm.1, s32[8,4,8]{2,1,0:T(4,128)} %bitcast.14, f32[3,64]{1,0:T(4,128)} %bitcast.15, s32[16]{0:T(128)} %partner_hbm.1, bf16[1024,256]{1,0:T(8,128)(2,1)} %constant.8.clone.high_hbm, ...), custom_call_target="tpu_custom_call" | custom-call | tf_op jit(solution)/shard_map/correlate/pallas_call | solution.py:761
  60.3 0.7 %copy.12 = f32[2,8,8,256]{3,2,1,0:T(8,128)} copy(f32[2,8,8,256]{3,2,1,0:T(8,128)S(1)} %bitcast.12) | data formatting | bytes 262144

commit v7 on v6

--- a/solution.py
+++ b/solution.py
@@ -360,8 +360,8 @@
     def start_phases(p):
         def one(r, _):
             c, s = cos_sin_turns(dsplat[p, pl.ds(r, 1), :] * channel)
-            base_c[r] = c
-            base_s[r] = s
+            base_c[p % 2, r] = c
+            base_s[p % 2, r] = s
             return 0
 
         lax.fori_loop(0, spectra, one, 0, unroll=8)
@@ -492,9 +492,9 @@
             def _():
                 wait_spectra(local, stations - TILE)
 
-            @pl.when(quarter == 0)
-            def _():
-                start_phases(p)
+            @pl.when((quarter == 1) & (p < mine - 1))
+            def _():
+                start_phases(p + 1)
 
         def rotate(n, _):
             for j in range(2):
@@ -504,8 +504,8 @@
                     tmp[j * depth + k] = xall[s, p, k, band(i), :].astype(jnp.float32)
                     real = tmp[j * depth + k, pl.ds(0, SUB, stride=2), :]
                     imag = tmp[j * depth + k, pl.ds(1, SUB, stride=2), :]
-                    c = base_c[r]
-                    sn = base_s[r]
+                    c = base_c[p % 2, r]
+                    sn = base_s[p % 2, r]
                     w = wide_w[r, at, :]
                     new_real = (w * (real * c + imag * sn)).astype(jnp.bfloat16).astype(jnp.float32)
                     new_imag = (w * (imag * c - real * sn)).astype(jnp.bfloat16).astype(jnp.float32)
@@ -515,8 +515,8 @@
                     yd[quarter, k, s] = new_real - new_imag
                     pc = step_c[p, pl.ds(r, 1), :]
                     ps = step_s[p, pl.ds(r, 1), :]
-                    base_c[r] = c * pc - sn * ps
-                    base_s[r] = sn * pc + c * ps
+                    base_c[p % 2, r] = c * pc - sn * ps
+                    base_s[p % 2, r] = sn * pc + c * ps
             return 0
 
         lax.fori_loop(0, (TILE if late else stations - TILE) // 2, rotate, 0)
@@ -598,8 +598,13 @@
                     def _():
                         scatter_copy(p, shift, "early", target, t).start()
 
-        if which != "early" and mine > 1:
-            @pl.when((quarter == QUARTERS - 1) & (p > 0))
+        if which == "all" and mine > 2:
+            @pl.when(((quarter == 1) & (p >= 2)) | ((quarter == 2) & (p == mine - 2)))
+            def _():
+                reduce_period(p - 3 + quarter)
+
+        if which == "late" and mine > 1:
+            @pl.when(quarter == QUARTERS - 1)
             def _():
                 reduce_period(p - 1)
 
@@ -634,6 +639,7 @@
 
         return 0
 
+    start_phases(0)
     own_copy.wait()
     if normal:
         lax.fori_loop(0, normal + ahead, step, 0)
@@ -784,8 +790,8 @@
             pltpu.VMEM((mine, spectra_rows, LANES), f32),
             pltpu.VMEM((mine, spectra_rows, LANES), f32),
             pltpu.VMEM((mine, spectra_rows, LANES), f32),
-            pltpu.VMEM((spectra_rows, SUB, LANES), f32),
-            pltpu.VMEM((spectra_rows, SUB, LANES), f32),
+            pltpu.VMEM((2, spectra_rows, SUB, LANES), f32),
+            pltpu.VMEM((2, spectra_rows, SUB, LANES), f32),
             pltpu.VMEM(high.shape, bf16),
             pltpu.VMEM(low.shape, bf16),
             pltpu.VMEM(pick_a.shape[1:], bf16),

time: 61.1 us -> 61.1 us (level)
  no operation moved by 1% of the time
where the time goes in v7:
time: 61.1 us; the launch traced here: 60.9 us
  Pallas kernels  60.3 us (99%)
  local copies, waits for them, and re-layouts  0.66 us (1%)
    pallas_call x1, Pallas kernels, per_device(): pl.pallas_call(functools.partial(kernel, (groups, owners, stations, perio...  60.3 us

profile of v7, /device:TPU:0, one launch (start us, length us, event | category | flops | bytes accessed | tf_op | source)
XLA Modules:
  0.0 60.9 jit_solution(8989829999385860569)
XLA Ops:
  0.0 60.3 %correlate.1 = f32[2,128,128]{2,1,0:T(8,128)S(1)} custom-call(bf16[8,8,4,64,128]{4,3,2,1,0:T(8,128)(2,1)} %bitcast.13, s32[8,8,4,32]{3,2,1,0:T(4,128)} %flags_hbm.1, s32[8,4,8]{2,1,0:T(4,128)} %bitcast.14, f32[3,64]{1,0:T(4,128)} %bitcast.15, s32[16]{0:T(128)} %partner_hbm.1, bf16[1024,256]{1,0:T(8,128)(2,1)} %constant.8.clone.high_hbm, ...), custom_call_target="tpu_custom_call" | custom-call | tf_op jit(solution)/shard_map/correlate/pallas_call | solution.py:767
  60.3 0.7 %copy.12 = f32[2,8,8,256]{3,2,1,0:T(8,128)} copy(f32[2,8,8,256]{3,2,1,0:T(8,128)S(1)} %bitcast.12) | data formatting | bytes 262144

commit v8 on v7

--- a/solution.py
+++ b/solution.py
@@ -284,7 +284,8 @@
     delay = (coef[0] + coef[1] * moment + coef[2] * moment * moment) * (0.5 / (blocks * LANES))
     dsend[...] = jnp.zeros_like(dsend)
     for g in range(groups):
-        dsend[g, :, :, :mine] = delay[:, :, g * mine : (g + 1) * mine]
+        pieces = [delay[l][:, g * mine : (g + 1) * mine] for l in range(local)]
+        dsend[g, :, : local * mine] = jnp.concatenate(pieces, axis=-1)
     tables[0].wait()
     for g in range(groups):
         pieces = [flags[:, g * mine + p].astype(jnp.float32) for p in range(mine)]
@@ -346,9 +347,10 @@
         for l in range(local):
             r = (g * local + (l + turn_by * min(g, 1)) % local) * depth
             wrow[r : r + depth, :] = wbuf[g, l].astype(jnp.float32)
-            d = dbuf[g, l]
+            d = dbuf[g]
             for p in range(mine):
-                dsplat[p, r : r + depth, :] = jnp.broadcast_to(d[:, p : p + 1], d.shape)
+                n = l * mine + p
+                dsplat[p, r : r + depth, :] = jnp.broadcast_to(d[:, n : n + 1], d.shape)
     c, s = cos_sin_turns(dsplat[...] * float(SUB * LANES))
     step_c[...] = c
     step_s[...] = s
@@ -609,7 +611,7 @@
                 reduce_period(p - 1)
 
     normal = steps - QUARTERS
-    ahead = 3 if normal else 0
+    ahead = 2 if normal else 0
 
     def step(m, _):
         stages = (normal + ahead) // ahead
@@ -752,7 +754,7 @@
     steps = mine * QUARTERS
     width = channels // QUARTERS
     lanes = LANES
-    assert channels == blocks * LANES and width == SUB * LANES and stations % TILE == 0 and mine * blocks <= lanes
+    assert channels == blocks * LANES and width == SUB * LANES and stations % TILE == 0 and mine * blocks <= lanes and local * mine <= lanes
 
     x = spectra.reshape(local, periods, depth, 2, blocks, LANES).transpose(0, 1, 2, 4, 3, 5)
     x = x.reshape(local, periods, depth, 2 * blocks, LANES)
@@ -776,9 +778,9 @@
             pltpu.SMEM(delay_model.shape[::-1], f32),
             pltpu.SMEM(partner_order.shape, i32),
             pltpu.VMEM((groups, local, depth, lanes), bf16),
-            pltpu.VMEM((groups, local, depth, LANES), f32),
+            pltpu.VMEM((groups, depth, LANES), f32),
             pltpu.VMEM((groups, local, depth, lanes), bf16),
-            pltpu.VMEM((groups, local, depth, LANES), f32),
+            pltpu.VMEM((groups, depth, LANES), f32),
             pltpu.VMEM((owners, groups, local, depth, lanes), bf16),
             pltpu.VMEM((stations, owners * depth, lanes), f32),
             pltpu.VMEM((spectra_rows, lanes), f32),

time: 61.1 us -> 60.8 us (level)
  no operation moved by 1% of the time
where the time goes in v8:
time: 60.8 us; the launch traced here: 60.6 us
  Pallas kernels  59.9 us (99%)
  local copies, waits for them, and re-layouts  0.66 us (1%)
    pallas_call x1, Pallas kernels, per_device(): pl.pallas_call(functools.partial(kernel, (groups, owners, stations, perio...  59.9 us

profile of v8, /device:TPU:0, one launch (start us, length us, event | category | flops | bytes accessed | tf_op | source)
XLA Modules:
  0.0 60.6 jit_solution(10761629605811623312)
XLA Ops:
  0.0 59.9 %correlate.1 = f32[2,128,128]{2,1,0:T(8,128)S(1)} custom-call(bf16[8,8,4,64,128]{4,3,2,1,0:T(8,128)(2,1)} %bitcast.13, s32[8,8,4,32]{3,2,1,0:T(4,128)} %flags_hbm.1, s32[8,4,8]{2,1,0:T(4,128)} %bitcast.14, f32[3,64]{1,0:T(4,128)} %bitcast.15, s32[16]{0:T(128)} %partner_hbm.1, bf16[1024,256]{1,0:T(8,128)(2,1)} %constant.8.clone.high_hbm, ...), custom_call_target="tpu_custom_call" | custom-call | tf_op jit(solution)/shard_map/correlate/pallas_call | solution.py:769
  60.0 0.7 %copy.12 = f32[2,8,8,256]{3,2,1,0:T(8,128)} copy(f32[2,8,8,256]{3,2,1,0:T(8,128)S(1)} %bitcast.12) | data formatting | bytes 262144
